TPU v7x, 256 devices: a whole 4x4x8 slice. The times are simulated.
256 devices in a mesh: dp: 64 (over x, z, core), tensor: 4 (over y).
Axes of the slice: x: 4, y: 4, z: 8, core: 2. Of those that a mesh axis runs over, the one named last changes fastest.
Arguments:
- gate_preactivation: bfloat16 [1024, 28672], P('dp', 'tensor'), may hold values from -6 to 6
- up_preactivation: bfloat16 [1024, 28672], P('dp', 'tensor'), may hold values from -6 to 6
- cotangent: bfloat16 [1024, 8192], P('dp'), may hold values from -0.1875 to 0.1875
- down_weight: bfloat16 [28672, 8192], P('tensor', 'dp'), may hold values from -0.03125 to 0.03125
- lowrank_factor_first: bfloat16 [28672, 64], P('tensor'), may hold values from -0.03125 to 0.03125
- lowrank_factor_second: bfloat16 [64, 8192], replicated, may hold values from -0.75 to 0.75
- sparse_block_values: bfloat16 [64, 4, 2, 128, 128], P('dp', 'tensor'), may hold values from -0.5 to 0.5
- slot_block_rows: int32 [64, 4, 2], P(None, 'tensor'), may hold values from 0 to 55, as said below
- slot_block_columns: int32 [64, 4, 2], P(None, 'tensor'), may hold values from 0 to 0
- owner_slot_counts: int32 [64, 4], P(None, 'tensor'), may hold values from 1 to 2, as said below
Outputs:
- mixed: bfloat16 [1024, 8192], P('tensor', 'dp')
- grad_a: float32 [28672, 64], P('tensor')
- grad_b: float32 [64, 8192], P(None, 'dp')
- grad_blocks: float32 [64, 4, 2, 128, 128], P('dp', 'tensor')
Inputs may be any that keep to these rules, and one draw needn't show every extreme that they name: `slot_block_rows`: the 2 slots of one owner name different blocks. `owner_slot_counts`: some owner has exactly 2 live slots.
All inputs are finite; a program needn't handle non-finite values.
Results may differ from a plain program's by a relative error of at most 0.0049.
Values may be sent and summed in bfloat16 or wider, within the bound.
No kernel may reach another device: no remote copies, remote signals or barrier semaphores. Data moves between devices by JAX's collectives and lax.ppermute only.
A program may use at most 128 MiB of HBM per device.

v0:
```python
import jax
import jax.numpy as jnp
from jax import lax
from jax.sharding import Mesh
from jax.sharding import PartitionSpec as P

DP = ("dp_0", "dp_1", "dp_2")


def split_up(array, dim, count):
    before, after = (array.shape[:dim], array.shape[dim + 1 :])
    return jnp.moveaxis(array.reshape(*before, count, -1, *after), dim, 0)


def sent_and_summed(array, axis, dim):
    blocks = split_up(array, dim, lax.axis_size(axis))
    arrived = lax.all_to_all(blocks, axis, split_axis=0, concat_axis=0, tiled=True)
    return arrived.sum(axis=0)


def sent_to_all(array, axis):
    count = lax.axis_size(axis)
    return lax.all_to_all(
        jnp.broadcast_to(array[None], (count, *array.shape)), axis, 0, 0, tiled=True
    )


def of_everyone(array, axis):
    return sent_to_all(array, axis).sum(axis=0)


def joined_along(blocks, dim):
    blocks = jnp.moveaxis(blocks, 0, dim)
    lengths = blocks.shape
    return blocks.reshape(*lengths[:dim], lengths[dim] * lengths[dim + 1], *lengths[dim + 2 :])


def collect(array, axis, dim):
    return joined_along(sent_to_all(array, axis), dim)


def all_blocks(array, axes, turns):
    blocks = array
    for k in turns:
        blocks = lax.all_gather(blocks, axes[k])
    done = turns[::-1]
    back = [done.index(k) for k in range(len(axes))]
    blocks = blocks.transpose(*back, *range(len(axes), blocks.ndim))
    return blocks.reshape(-1, *array.shape)


def gathered_by_axis(array, axes, turns, dim):
    return joined_along(all_blocks(array, axes, turns), dim)


def column_view(cotangent):
    return lax.all_to_all(cotangent, DP, split_axis=1, concat_axis=0, tiled=True)


def shards(
    gate_preactivation,
    up_preactivation,
    cotangent,
    down_weight,
    lowrank_factor_first,
    lowrank_factor_second,
    sparse_block_values,
    slot_block_rows,
    slot_block_columns,
    owner_slot_counts,
):
    data_parallel_index = lax.axis_index(DP)
    column_offset = down_weight.shape[1]
    side = sparse_block_values.shape[-1]
    slots = sparse_block_values.shape[2]
    per_col = column_offset // side
    hidden_activation = (
        jax.nn.silu(gate_preactivation.astype(jnp.float32)) * up_preactivation.astype(jnp.float32)
    ).astype(jnp.bfloat16)
    hidden_gathered = lax.all_gather(hidden_activation, DP, axis=0, tiled=True)
    tok_all = hidden_gathered.shape[0]
    rows_all = slot_block_rows[:, 0, :]
    cols_all = slot_block_columns[:, 0, :]
    live_all = (
        jnp.arange(slots, dtype=jnp.int32)[None, :] < owner_slot_counts[:, 0][:, None]
    ).astype(jnp.float32)
    own_rows = lax.dynamic_index_in_dim(rows_all, data_parallel_index, 0, keepdims=False)
    own_cols = lax.dynamic_index_in_dim(cols_all, data_parallel_index, 0, keepdims=False)
    own_live = lax.dynamic_index_in_dim(live_all, data_parallel_index, 0, keepdims=False)
    factor_b_window = lax.dynamic_slice_in_dim(
        lowrank_factor_second, data_parallel_index * column_offset, column_offset, 1
    ).astype(jnp.float32)
    col_pick = (own_cols[:, None] == jnp.arange(per_col, dtype=jnp.int32)[None, :]).astype(
        jnp.float32
    ) * own_live[:, None]
    blocks = sparse_block_values[0, 0]
    owned_hidden = jnp.stack(
        [
            lax.dynamic_slice_in_dim(hidden_gathered, own_rows[slot] * side, side, 1)
            for slot in range(slots)
        ],
        axis=1,
    )
    total = jnp.dot(hidden_gathered, down_weight, preferred_element_type=jnp.float32)
    lowrank_token_rows = jnp.dot(
        hidden_gathered, lowrank_factor_first, preferred_element_type=jnp.float32
    )
    total = total + jnp.dot(lowrank_token_rows, factor_b_window, precision=lax.Precision.HIGHEST)
    local = jnp.einsum("tkc,kcd->tkd", owned_hidden, blocks, preferred_element_type=jnp.float32)
    spread = jnp.einsum("tkd,kn->tnd", local, col_pick, precision=lax.Precision.HIGHEST)
    summed = sent_and_summed(
        total
        + spread.reshape(
            tok_all // lax.axis_size("tensor") * lax.axis_size("tensor"), column_offset
        ),
        "tensor",
        0,
    )
    mixed = summed.astype(jnp.bfloat16)
    cotangent_lowrank = lax.dot_general(
        cotangent,
        lowrank_factor_second,
        (((1,), (1,)), ((), ())),
        preferred_element_type=jnp.float32,
    ).astype(jnp.bfloat16)
    lowrank_local_part = jnp.dot(
        hidden_activation, lowrank_factor_first, preferred_element_type=jnp.float32
    )
    cot_cols = None
    cot_cols = column_view(cotangent)
    low_full = of_everyone(lowrank_local_part, "tensor")
    low_all = collect(low_full, DP, 0)
    grad_b = lax.dot_general(
        low_all,
        cot_cols.astype(jnp.float32),
        (((0,), (0,)), ((), ())),
        precision=lax.Precision.HIGHEST,
    )
    cot_all = gathered_by_axis(cotangent_lowrank, DP, (0, 1, 2), 0)
    grad_a = lax.dot_general(
        hidden_gathered, cot_all, (((0,), (0,)), ((), ())), preferred_element_type=jnp.float32
    )
    pick_own = (own_cols[:, None] == jnp.arange(per_col, dtype=jnp.int32)[None, :]).astype(
        jnp.bfloat16
    )
    picked_c = jnp.einsum(
        "tnd,kn->tkd",
        cot_cols.reshape(tok_all, per_col, side),
        pick_own,
        preferred_element_type=jnp.float32,
    ).astype(jnp.bfloat16)
    owned = jnp.einsum("tkc,tkd->kcd", owned_hidden, picked_c, preferred_element_type=jnp.float32)
    grad_blocks = (owned * own_live[:, None, None])[None, None]
    return (mixed, grad_a, grad_b, grad_blocks)


def solution(mesh):
    finer = Mesh(
        mesh.devices.reshape(4, 8, 2, mesh.shape["tensor"]), ("dp_0", "dp_1", "dp_2", "tensor")
    )
    in_specs = (
        P(DP, "tensor"),
        P(DP, "tensor"),
        P(DP, None),
        P("tensor", DP),
        P("tensor", None),
        P(),
        P(DP, "tensor", None, None, None),
        P(None, "tensor", None),
        P(None, "tensor", None),
        P(None, "tensor"),
    )
    out_specs = (P("tensor", DP), P("tensor", None), P(None, DP), P(DP, "tensor", None, None, None))
    return jax.shard_map(
        shards, mesh=finer, in_specs=in_specs, out_specs=out_specs, check_vma=False
    )
```

profile of v0, /device:TPU:1, one launch (start us, length us, event | category | flops | bytes accessed | tf_op | source)
XLA Modules:
  0.0 160.6 jit_solution(10013752832817767674)
XLA Ops:
  7.2 0.0 copy-start
  7.2 0.0 copy-start.2
  7.2 0.0 all-gather.5.cloned.1.call-start
  7.2 2.1 %fusion.12 = bf16[16,7168]{1,0:T(8,128)(2,1)} fusion(bf16[16,7168]{1,0:T(8,128)(2,1)} %param.11, bf16[16,7168]{1,0:T(8,128)(2,1)} %param.10), kind=kLoop, calls=%fused_computation.20 | loop fusion | flops 917504 | bytes 688128 | tf_op jit(solution)/shard_map/convert_element_type | solution.py:79
  9.3 0.0 all-gather.5.cloned.1.call-update
  9.3 1.6 %fusion.27 = f32[16,64]{1,0:T(8,128)S(1)} fusion(bf16[16,7168]{1,0:T(8,128)(2,1)} %fusion.12, bf16[7168,64]{0,1:T(8,128)(2,1)} %param.14), kind=kOutput, calls=%fused_computation.43 | convolution fusion | flops 14680064 | bytes 1150976 | tf_op jit(solution)/shard_map/dot_general | solution.py:126
  11.0 0.7 reshape.70
  11.7 5.0 %all-to-all-start.1 = ((f32[4,1,1024]{2,1,0:T(1,128)}), f32[4,1,1024]{2,1,0:T(1,128)S(1)}, u32[]{:S(2)}, u32[]{:S(2)}) async-start(f32[4,1,1024]{2,1,0:T(1,128)} %reshape.70), calls=%async_computation.1 | async-start | bytes 32768 | tf_op jit(solution)/shard_map/all_to_all | solution.py:23
  16.7 1.7 %copy_bitcast_fusion = bf16[16,64,128]{2,0,1:T(8,128)(2,1)} fusion(bf16[16,8192]{1,0:T(8,128)(2,1)} %param.12), kind=kLoop, calls=%fused_computation.21 | loop fusion | bytes 524288 | tf_op jit(solution)/shard_map/all_to_all | solution.py:57
  18.4 2.5 %all-to-all-done.1 = f32[4,1,1024]{2,1,0:T(1,128)S(1)} async-done(((f32[4,1,1024]{2,1,0:T(1,128)}), f32[4,1,1024]{2,1,0:T(1,128)S(1)}, u32[]{:S(2)}, u32[]{:S(2)}) %all-to-all-start.1) | async-done | bytes 16416 | tf_op jit(solution)/shard_map/all_to_all | solution.py:23
  20.9 13.6 %all-to-all-start.3 = ((bf16[16,64,128]{2,0,1:T(8,128)(2,1)}), bf16[16,64,128]{2,0,1:T(8,128)(2,1)S(1)}, u32[]{:S(2)}, u32[]{:S(2)}) async-start(bf16[16,64,128]{2,0,1:T(8,128)(2,1)} %copy_bitcast_fusion), calls=%async_computation.3 | async-start | bytes 524288 | tf_op jit(solution)/shard_map/all_to_all | solution.py:57
  34.5 0.8 constant_dynamic-slice_fusion
  35.3 1.7 %convolution_convert_fusion = bf16[16,64]{1,0:T(8,128)(2,1)S(1)} fusion(bf16[16,8192]{1,0:T(8,128)(2,1)} %param.12, bf16[64,8192]{1,0:T(8,128)(2,1)} %param.15), kind=kOutput, calls=%fused_computation.6 | convolution fusion | flops 16778240 | bytes 1312768 | tf_op jit(solution)/shard_map/dot_general | solution.py:120
  36.9 0.6 broadcast.31
  37.5 0.7 reduce.2
  38.2 0.1 reshape.71
  38.4 1.0 reshape.72
  39.4 9.2 %all-to-all-done.3 = bf16[16,64,128]{2,0,1:T(8,128)(2,1)S(1)} async-done(((bf16[16,64,128]{2,0,1:T(8,128)(2,1)}), bf16[16,64,128]{2,0,1:T(8,128)(2,1)S(1)}, u32[]{:S(2)}, u32[]{:S(2)}) %all-to-all-start.3) | async-done | bytes 262176 | tf_op jit(solution)/shard_map/all_to_all | solution.py:57
  48.6 6.4 %all-to-all-start.2 = ((f32[64,1,1024]{2,1,0:T(1,128)}), f32[64,1,1024]{2,1,0:T(1,128)}, u32[]{:S(2)}, u32[]{:S(2)}) async-start(f32[64,1,1024]{2,1,0:T(1,128)} %reshape.72), calls=%async_computation.2 | async-start | bytes 524288 | tf_op jit(solution)/shard_map/all_to_all | solution.py:23
  55.0 0.5 fusion.23
  56.8 1.2 dynamic-slice.2
  58.1 0.9 compare_reduce_fusion
  58.9 10.5 %all-gather = bf16[64,64]{1,0:T(8,128)(2,1)S(1)} all-gather(bf16[16,64]{1,0:T(8,128)(2,1)S(1)} %convolution_convert_fusion), channel_id=2, replica_groups=mesh['dp_0'=4,'dp_1'=8,'dp_2'=2,'tensor'=4] {'dp_0'}, dimensions={0}, use_global_device_ids=true | all-gather | bytes 10240 | tf_op jit(solution)/shard_map/all_gather | solution.py:45
  69.4 22.0 %all-gather.1 = bf16[32,16,64]{2,1,0:T(8,128)(2,1)S(1)} all-gather(bf16[4,16,64]{2,1,0:T(8,128)(2,1)S(1)} %bitcast.65), channel_id=3, replica_groups=mesh['dp_0'=4,'dp_1'=8,'dp_2'=2,'tensor'=4] {'dp_1'}, dimensions={0}, use_global_device_ids=true | all-gather | bytes 73728 | tf_op jit(solution)/shard_map/all_gather | solution.py:45
  91.3 8.6 %all-gather.2 = bf16[16,4,16,64]{3,2,1,0:T(8,128)(2,1)S(1)} all-gather(bf16[8,4,16,64]{3,2,1,0:T(8,128)(2,1)S(1)} %bitcast.63), channel_id=4, replica_groups=mesh['dp_0'=4,'dp_1'=8,'dp_2'=2,'tensor'=4] {'dp_2'}, dimensions={0}, use_global_device_ids=true | all-gather | bytes 196608 | tf_op jit(solution)/shard_map/all_gather | solution.py:45
  100.0 0.7 fusion.17
  100.7 0.9 bitcast_convert_fusion
  101.5 0.0 all-to-all-done.2
  101.6 2.2 %reduce.3 = f32[64,1024]{1,0:T(8,128)S(1)} reduce(f32[64,1,1024]{2,1,0:T(1,128)} %all-to-all-done.2, f32[]{:T(128)} %broadcast.31), dimensions={1}, to_apply=%all_to_all.23.reduce_sub_computation | reduce | bytes 524292 | tf_op jit(solution)/shard_map/all_to_all | solution.py:23
  103.8 0.9 reshape.73
  104.7 2.2 %convolution_bitcast_fusion.1 = f32[64,128]{1,0:T(8,128)} fusion(f32[64,16,64]{2,1,0:T(8,128)} %reshape.73, bf16[16,64,128]{2,0,1:T(8,128)(2,1)S(1)} %all-to-all-done.3), kind=kOutput, calls=%fused_computation.5 | convolution fusion | flops 100663296 | bytes 557056 | tf_op jit(solution)/shard_map/dot_general | solution.py:133
  107.0 5.6 %all-gather.5.cloned.1.call-done = bf16[1024,7168]{1,0:T(8,128)(2,1)} async-done(((bf16[16,7168]{1,0:T(8,128)(2,1)}), bf16[1024,7168]{1,0:T(8,128)(2,1)}) %all-gather.5.cloned.1.call-update) | async-done | bytes 14680080 | tf_op jit(solution)/shard_map/all_gather | solution.py:80
  112.6 0.0 copy-start.1
  112.6 1.2 dynamic-slice_bitcast_fusion.1
  113.8 1.3 convolution_bitcast_fusion
  115.2 7.9 %fusion.2 = f32[1,1024,128]{2,0,1:T(1,128)S(1)} fusion(f32[1024,2,128]{2,0,1:T(8,128)S(1)} %convolution_bitcast_fusion, pred[2]{0:T(512)(128)(4,1)S(1)} %compare_reduce_fusion, s32[1]{0:T(128)} %dynamic-slice.2), kind=kOutput, calls=%fused_computation.8 | convolution fusion | flops 3145734 | bytes 1572870 | tf_op jit(solution)/shard_map/tkd,kn->tnd/dot_general | solution.py:110
  123.1 0.0 copy-done.2
  123.1 9.7 %fusion.25 = f32[1024,64]{0,1:T(8,128)S(1)} fusion(bf16[1024,7168]{1,0:T(8,128)(2,1)} %all-gather.5.cloned.1.call-done, bf16[7168,64]{0,1:T(8,128)(2,1)S(1)} %copy-done.2), kind=kOutput, calls=%fused_computation.41 | convolution fusion | flops 939524096 | bytes 15859712 | tf_op jit(solution)/shard_map/dot_general | solution.py:105
  132.8 0.0 copy-done
  132.8 0.0 copy-done.1
  132.8 4.0 %fusion.24 = f32[1024,128]{1,0:T(8,128)S(1)} fusion(bf16[1024,7168]{1,0:T(8,128)(2,1)S(1)} %copy-done.1, bf16[7168,128]{1,0:T(8,128)(2,1)S(1)} %copy-done), kind=kOutput, calls=%fused_computation.40 | convolution fusion | flops 1879048192 | bytes 17039360 | tf_op jit(solution)/shard_map/dot_general | solution.py:104
  136.8 2.2 %fusion = f32[1024,128]{1,0:T(8,128)} fusion(f32[1024,128]{1,0:T(8,128)S(1)} %bitcast.64, f32[1024,128]{1,0:T(8,128)S(1)} %fusion.24, f32[1024,64]{0,1:T(8,128)S(1)} %fusion.25, bf16[64,8192]{1,0:T(8,128)(2,1)} %param.15, s32[]{:T(128)S(6)} %select_n.16), kind=kOutput, calls=%fused_computation.2 | convolution fusion | flops 100925440 | bytes 1851396 | tf_op jit(solution)/shard_map/dot_general | solution.py:108
  138.9 3.9 %all-to-all-start = ((f32[4,256,128]{2,1,0:T(8,128)}), f32[4,256,128]{2,1,0:T(8,128)S(1)}, u32[]{:S(2)}, u32[]{:S(2)}) async-start(f32[4,256,128]{2,1,0:T(8,128)} %bitcast.12), calls=%async_computation | async-start | bytes 1048576 | tf_op jit(solution)/shard_map/all_to_all | solution.py:17
  142.9 0.0 copy-start.3
  142.9 9.2 %fusion.26 = f32[7168,64]{0,1:T(8,128)} fusion(bf16[1024,7168]{1,0:T(8,128)(2,1)} %all-gather.5.cloned.1.call-done, bf16[1024,64]{1,0:T(8,128)(2,1)S(1)} %bitcast.61), kind=kOutput, calls=%fused_computation.42 | convolution fusion | flops 939524096 | bytes 16646144 | tf_op jit(solution)/shard_map/dot_general | solution.py:140
  152.1 0.0 copy-done.3
  152.1 1.0 fusion.1
  153.1 0.0 all-to-all-done
  153.1 0.7 reduce_sum.18
  (5 shorter events, 0.1 us)
Async XLA Ops:
  7.2 125.6 %copy-start = (bf16[7168,128]{1,0:T(8,128)(2,1)S(1)}, bf16[7168,128]{1,0:T(8,128)(2,1)}, u32[]{:S(2)}) copy-start(bf16[7168,128]{1,0:T(8,128)(2,1)} %param.13) | copy-start | bytes 5505028
  7.2 115.9 %copy-start.2 = (bf16[7168,64]{0,1:T(8,128)(2,1)S(1)}, bf16[7168,64]{0,1:T(8,128)(2,1)}, u32[]{:S(2)}) copy-start(bf16[7168,64]{0,1:T(8,128)(2,1)} %param.14) | copy-start | bytes 2752516
  7.2 105.4 %all-gather.5.cloned.1.call-start = ((), (), s32[]{:S(2)}) async-start(), calls=%async_computation.4 | async-start | bytes 14909440 | tf_op jit(solution)/shard_map/all_gather | solution.py:80
  11.7 9.2 %all-to-all-start.1 = ((f32[4,1,1024]{2,1,0:T(1,128)}), f32[4,1,1024]{2,1,0:T(1,128)S(1)}, u32[]{:S(2)}, u32[]{:S(2)}) async-start(f32[4,1,1024]{2,1,0:T(1,128)} %reshape.70), calls=%async_computation.1 | async-start | bytes 32768 | tf_op jit(solution)/shard_map/all_to_all | solution.py:23
  20.9 27.7 %all-to-all-start.3 = ((bf16[16,64,128]{2,0,1:T(8,128)(2,1)}), bf16[16,64,128]{2,0,1:T(8,128)(2,1)S(1)}, u32[]{:S(2)}, u32[]{:S(2)}) async-start(bf16[16,64,128]{2,0,1:T(8,128)(2,1)} %copy_bitcast_fusion), calls=%async_computation.3 | async-start | bytes 524288 | tf_op jit(solution)/shard_map/all_to_all | solution.py:57
  48.6 53.0 %all-to-all-start.2 = ((f32[64,1,1024]{2,1,0:T(1,128)}), f32[64,1,1024]{2,1,0:T(1,128)}, u32[]{:S(2)}, u32[]{:S(2)}) async-start(f32[64,1,1024]{2,1,0:T(1,128)} %reshape.72), calls=%async_computation.2 | async-start | bytes 524288 | tf_op jit(solution)/shard_map/all_to_all | solution.py:23
  112.6 20.2 %copy-start.1 = (bf16[1024,7168]{1,0:T(8,128)(2,1)S(1)}, bf16[1024,7168]{1,0:T(8,128)(2,1)}, u32[]{:S(2)}) copy-start(bf16[1024,7168]{1,0:T(8,128)(2,1)} %all-gather.5.cloned.1.call-done) | copy-start | bytes 44040196
  138.9 14.2 %all-to-all-start = ((f32[4,256,128]{2,1,0:T(8,128)}), f32[4,256,128]{2,1,0:T(8,128)S(1)}, u32[]{:S(2)}, u32[]{:S(2)}) async-start(f32[4,256,128]{2,1,0:T(8,128)} %bitcast.12), calls=%async_computation | async-start | bytes 1048576 | tf_op jit(solution)/shard_map/all_to_all | solution.py:17
  142.9 9.2 %copy-start.3 = (f32[1024,128]{1,0:T(8,128)S(1)}, f32[1024,128]{1,0:T(8,128)}, u32[]{:S(2)}) copy-start(f32[1024,128]{1,0:T(8,128)} %bitcast_convert_fusion) | copy-start | bytes 1572868
Sparse Core Ops, SparseCore 0:
  10.7 101.7 all-gather.4
where the time goes:
time: 161 us
  blocking collectives  41 us (25%)
  matrix products  40.9 us (25%)
  starting transfers between devices  29 us (18%)
  waiting for transfers between devices  17.4 us (11%)
  between operations  15.5 us (10%)
  local copies, waits for them, and re-layouts  8.89 us (6%)
  other arithmetic  8 us (5%)
    all_gather x3, blocking collectives, all_blocks(): blocks = lax.all_gather(blocks, axes[k])  41 us
    all_to_all x1, starting transfers between devices, column_view(): lax.all_to_all(cotangent, DP, split_axis=1, concat_axis=0, tiled=True)  13.6 us
    all_to_all x2, starting transfers between devices, sent_to_all(): lax.all_to_all(jnp.broadcast_to(array[None], (count, *array.shape)), axis...  11.4 us
    dot_general x1, matrix products, shards(): jnp.dot(hidden_gathered, lowrank_factor_first, preferred_element_type=jnp...  9.72 us
    all_to_all x1, waiting for transfers between devices, column_view(): lax.all_to_all(cotangent, DP, split_axis=1, concat_axis=0, tiled=True)  9.2 us
    dot_general x1, matrix products, shards(): lax.dot_general(hidden_gathered, cot_all, (((0,), (0,)), ((), ())), prefe...  9.19 us
    dot_general x1, matrix products, shards(): jnp.einsum('tkd,kn->tnd', local, col_pick, precision=lax.Precision.HIGHEST)  7.9 us
    all_gather x1, waiting for transfers between devices, shards(): hidden_gathered = lax.all_gather(hidden_activation, DP, axis=0, tiled=True)  5.64 us
  transfers between devices with their start and end apart: 5, of which 3 were waited for; matrix products, arithmetic and copies ran while one was open for 18% of the time, Pallas kernels for 0%

commit v1 on v0

v1 whole, which is shorter than its diff:
```python
import functools

import jax
import jax.numpy as jnp
from jax import lax
from jax.experimental import pallas as pl
from jax.experimental.pallas import tpu as pltpu
from jax.sharding import Mesh
from jax.sharding import PartitionSpec as P


DP = ("x", "z", "c")
NX, NZ = 4, 8
bf = jnp.bfloat16
f32 = jnp.float32
CA = 3584
BLK = 1792
BIG = 60
XS = (0, -1, 1, 2)
ZS = (0, -1, 1, -2, 2, -3, 3, 4)


def shift(a, axis, k):
    n = lax.axis_size(axis)
    return lax.ppermute(a, axis, [(i, (i + k) % n) for i in range(n)])


def tn(a, b):
    return lax.dot_general(a, b, (((0,), (0,)), ((), ())), preferred_element_type=f32)


def kernel_stack(n, *refs):
    for k in range(n):
        refs[n + k // (n // 2)][k % (n // 2)] = refs[k][...]


def stack(parts):
    vm = pl.BlockSpec(memory_space=pltpu.VMEM)
    n = len(parts)
    half = jax.ShapeDtypeStruct((n // 2, *parts[0].shape), parts[0].dtype)
    return pl.pallas_call(
        functools.partial(kernel_stack, n),
        in_specs=[vm] * n,
        out_specs=[vm] * 2,
        out_shape=[half] * 2,
        compiler_params=params(8),
        name="stack",
    )(*parts)


def kernel_prep(s_ref, w_ref, wo_ref, at_ref, b_ref, sp_ref, spo_ref, out_ref):
    i = pl.program_id(0)
    own = s_ref[2]
    ab = tn(at_ref[...], b_ref[...])
    rows = out_ref.shape[0]
    for c in range(2):
        cols = slice(c * 128, (c + 1) * 128)

        @pl.when(own == c)
        def _():
            out_ref[:, cols] = (w_ref[...].astype(f32) + ab[:, cols]).astype(bf)

        @pl.when(own != c)
        def _():
            out_ref[:, cols] = (wo_ref[...].astype(f32) + ab[:, cols]).astype(bf)

    for j in range(4):
        at = s_ref[3 + j] * 128 - i * rows

        @pl.when((at >= 0) & (at < rows) & (s_ref[7 + j] > 0))
        def _():
            sp = sp_ref[j] if j < 2 else spo_ref[j - 2]
            c = own if j < 2 else 1 - own
            here = (pl.ds(pl.multiple_of(at, 128), 128), pl.ds(pl.multiple_of(c * 128, 128), 128))
            out_ref[here] = (out_ref[here].astype(f32) + sp.astype(f32)).astype(bf)


def assemble(scr, ref_list, places, xi, zi):
    for ref, place in zip(ref_list, places):
        for k, (dx, dz) in enumerate(place):
            row = (lax.rem(xi + dx + NX, NX) * NZ + lax.rem(zi + dz + NZ, NZ)) * 16
            scr[pl.ds(pl.multiple_of(row, 16), 16), :] = ref[k]


def kernel_a(places, n, s_ref, *refs):
    chunks, ext = refs[:n], refs[n : 2 * n]
    w_ref, cot_ref, out_ref, ga_ref, clt_ref, low_ref, gs_ref, scr, ext_scr = refs[2 * n :]
    i = pl.program_id(0)
    xi, zi = s_ref[0], s_ref[1]

    @pl.when(i == 0)
    def _():
        assemble(ext_scr, ext, places, xi, zi)
        low_ref[...] = ext_scr[...]
        clt_ref[...] = ext_scr[...].astype(f32).T.astype(bf)
        gs_ref[...] = jnp.zeros_like(gs_ref)

    assemble(scr, chunks, places, xi, zi)
    h = scr[...]
    part = jnp.dot(h, w_ref[...], preferred_element_type=f32)

    @pl.when(i == 0)
    def _():
        out_ref[...] = part

    @pl.when(i > 0)
    def _():
        out_ref[...] += part

    ga_ref[...] = jnp.dot(clt_ref[:64, :], h, preferred_element_type=f32)
    picks(i, 0, s_ref, scr, cot_ref, gs_ref)


def kernel_b(places, n, s_ref, *refs):
    chunks = refs[:n]
    w_ref, cot_ref, outa_ref, clt_ref, low_ref, gsa_ref, send_ref, ga_ref, gs_ref, scr, acc = refs[n:]
    i = pl.program_id(0)
    xi, zi = s_ref[0], s_ref[1]
    assemble(scr, chunks, places, xi, zi)
    h = scr[...]
    part = jnp.dot(h, w_ref[...], preferred_element_type=f32)

    @pl.when(i == 0)
    def _():
        acc[...] = outa_ref[...] + part
        gs_ref[...] = gsa_ref[...]

    @pl.when(i == pl.num_programs(0) - 1)
    def _():
        out = acc[...] + part
        gb = tn(low_ref[...], cot_ref[...])[64:]
        for c in range(2):
            for y in range(4):
                send_ref[c * 4 + y, :128, :] = out[y * 128 : (y + 1) * 128, c * 128 : (c + 1) * 128]
                send_ref[c * 4 + y, 128:, :] = gb[:, c * 128 : (c + 1) * 128]

    ga_ref[...] = jnp.dot(clt_ref[:64, :], h, preferred_element_type=f32)
    picks(i, CA // 128, s_ref, scr, cot_ref, gs_ref)


def picks(i, base, s_ref, scr, cot_ref, gs_ref):
    for j in range(4):
        at = (s_ref[3 + j] - base) * 128 - i * BLK

        @pl.when((at >= 0) & (at < BLK))
        def _():
            c = s_ref[2] if j < 2 else 1 - s_ref[2]
            cot = cot_ref[:, pl.ds(pl.multiple_of(c * 128, 128), 128)]
            gs_ref[j] = tn(scr[:, pl.ds(pl.multiple_of(at, 128), 128)], cot)


def kernel_final(got_ref, mixed_ref, gb_ref):
    acc = None
    for c in range(2):
        s = got_ref[c * 4]
        for y in range(1, 4):
            s = s + got_ref[c * 4 + y]
        for z in range(NZ):
            mixed_ref[z, c] = s[z * 16 : (z + 1) * 16].astype(bf)
        acc = s[128:] if acc is None else acc + s[128:]
    gb_ref[...] = acc


def kernel_add(x_ref, y_ref, o_ref):
    o_ref[...] = x_ref[...] + y_ref[...]


def kernel_add_to(_, x_ref, y_ref, o_ref):
    o_ref[...] = x_ref[...] + y_ref[...]


def params(mib=24):
    return pltpu.CompilerParams(vmem_limit_bytes=mib << 20)


def shards(gate, up, cot, w, a, b, sbv, rows, cols, counts):
    xi, zi, ci = lax.axis_index("x"), lax.axis_index("z"), lax.axis_index("c")
    chip = xi * NZ + zi
    K = w.shape[0]
    CB = K - CA
    first = ci == 0
    hid = (jax.nn.silu(gate.astype(f32)) * up.astype(f32)).astype(bf)
    own_b = hid[:, CA:]
    cl = lax.dot_general(cot, b, (((1,), (1,)), ((), ())), preferred_element_type=f32).astype(bf)
    lo = jnp.dot(hid, a, preferred_element_type=f32).astype(bf)
    own_a = jnp.concatenate([hid[:, :CA], cl, lo], axis=1)
    fb, bb = [own_b], [own_b]
    for _ in range(1, 4):
        fb.append(shift(fb[-1], "z", 1))
        bb.append(shift(bb[-1], "z", -1))
    sb = stack([own_b, fb[1], bb[1], fb[2], bb[2], fb[3], bb[3], shift(fb[3], "z", 1)])
    sa = stack([own_a, shift(own_a, "x", 1), shift(own_a, "x", -1), shift(own_a, "x", 2)])
    chunks_a, places_a = list(sa), [[(x, 0) for x in XS[:2]], [(x, 0) for x in XS[2:]]]
    f, r = list(sa), list(sa)
    for k in range(1, 5):
        for h in (0, 1):
            if k < 4 or h == 0:
                f[h] = shift(f[h], "z", 1)
                chunks_a.append(f[h])
                places_a.append([(x, -k) for x in XS[2 * h : 2 * h + 2]])
        for h in (1, 0):
            if k < 4 or h == 1:
                r[h] = shift(r[h], "z", -1)
                chunks_a.append(r[h])
                places_a.append([(x, k) for x in XS[2 * h : 2 * h + 2]])
    xf = [shift(sb[0], "x", 1), shift(sb[1], "x", 1)]
    xb = [shift(sb[0], "x", -1), shift(sb[1], "x", -1)]
    chunks_b = [*sb, *xf, *xb, shift(xf[0], "x", 1), shift(xb[1], "x", -1)]
    zs = [list(ZS[:4]), list(ZS[4:])]
    places_b = [[(x, z) for z in zs[h]] for x in XS for h in (0, 1)]
    sp = sbv[0, 0]
    w_o = shift(w, "c", 1)
    sp_o = shift(sp, "c", 1)
    b2 = lax.dynamic_slice_in_dim(b, chip * 256, 256, 1)
    r2 = lax.dynamic_slice_in_dim(rows[:, 0, :], chip * 2, 2, 0)
    live = jnp.arange(2, dtype=jnp.int32)[None, :] < lax.dynamic_slice_in_dim(counts[:, 0], chip * 2, 2, 0)[:, None]
    rel = jnp.where(first, r2, r2[::-1])
    rlive = jnp.where(first, live, live[::-1])
    scal = jnp.concatenate(
        [jnp.stack([xi, zi, ci]).astype(jnp.int32), rel.reshape(4), rlive.astype(jnp.int32).reshape(4)]
    )
    cc = lax.all_to_all(cot.reshape(16, 32, 256), ("x", "z"), split_axis=1, concat_axis=0)
    cc = cc.reshape(512, 256)

    def col(shape, off=0):
        return pl.BlockSpec(shape, lambda i, s: (0,) * (len(shape) - 1) + (i + off,))

    def whole(shape, at=None):
        return pl.BlockSpec(shape, lambda i, s: at or (0,) * len(shape))

    na, nb = len(chunks_a), len(chunks_b)
    cost = pl.CostEstimate(flops=2 * 512 * CA * 384, bytes_accessed=12 << 20, transcendentals=0)
    weff = pl.pallas_call(
        kernel_prep,
        grid_spec=pltpu.PrefetchScalarGridSpec(
            num_scalar_prefetch=1,
            grid=(K // BLK,),
            in_specs=[
                pl.BlockSpec((BLK, 128), lambda i, s: (i, 0)),
                pl.BlockSpec((BLK, 128), lambda i, s: (i, 0)),
                col((64, BLK)),
                whole((64, 256)),
                whole((2, 128, 128)),
                whole((2, 128, 128)),
            ],
            out_specs=pl.BlockSpec((BLK, 256), lambda i, s: (i, 0)),
        ),
        out_shape=jax.ShapeDtypeStruct((K, 256), bf),
        compiler_params=params(BIG),
        cost_estimate=pl.CostEstimate(flops=1 << 28, bytes_accessed=8 << 20, transcendentals=0),
        name="prep",
    )(scal, w, w_o, a.T, b2, sp, sp_o)
    out_a, ga_a, clt, low, gs_a = pl.pallas_call(
        functools.partial(kernel_a, places_a, na),
        grid_spec=pltpu.PrefetchScalarGridSpec(
            num_scalar_prefetch=1,
            grid=(CA // BLK,),
            in_specs=[col((x.shape[0], 16, BLK)) for x in chunks_a]
            + [whole((x.shape[0], 16, 128), (0, 0, CA // 128)) for x in chunks_a]
            + [pl.BlockSpec((BLK, 256), lambda i, s: (i, 0)), whole((512, 256))],
            out_specs=[whole((512, 256)), col((64, BLK)), whole((128, 512)), whole((512, 128)), whole((4, 128, 128))],
            scratch_shapes=[pltpu.VMEM((512, BLK), bf), pltpu.VMEM((512, 128), bf)],
        ),
        out_shape=[
            jax.ShapeDtypeStruct((512, 256), f32),
            jax.ShapeDtypeStruct((64, CA), f32),
            jax.ShapeDtypeStruct((128, 512), bf),
            jax.ShapeDtypeStruct((512, 128), bf),
            jax.ShapeDtypeStruct((4, 128, 128), f32),
        ],
        compiler_params=params(BIG),
        cost_estimate=cost,
        name="colour_a",
    )(scal, *chunks_a, *chunks_a, weff, cc)
    send, ga_b, gs = pl.pallas_call(
        functools.partial(kernel_b, places_b, nb),
        grid_spec=pltpu.PrefetchScalarGridSpec(
            num_scalar_prefetch=1,
            grid=(CB // BLK,),
            in_specs=[col((x.shape[0], 16, BLK)) for x in chunks_b]
            + [
                pl.BlockSpec((BLK, 256), lambda i, s: (i + CA // BLK, 0)),
                whole((512, 256)),
                whole((512, 256)),
                whole((128, 512)),
                whole((512, 128)),
                whole((4, 128, 128)),
            ],
            out_specs=[whole((8, 192, 128)), col((64, BLK)), whole((4, 128, 128))],
            scratch_shapes=[pltpu.VMEM((512, BLK), bf), pltpu.VMEM((512, 256), f32)],
        ),
        out_shape=[
            jax.ShapeDtypeStruct((8, 192, 128), f32),
            jax.ShapeDtypeStruct((64, CB), f32),
            jax.ShapeDtypeStruct((4, 128, 128), f32),
        ],
        compiler_params=params(BIG),
        cost_estimate=cost,
        name="colour_b",
    )(scal, *chunks_b, weff, cc, out_a, clt, low, gs_a)
    vm = pl.BlockSpec(memory_space=pltpu.VMEM)
    got = lax.all_to_all(send, ("c", "y"), 0, 0, tiled=True)
    gsum = gs[:2] + shift(gs[2:], "c", 1)
    grad_blocks = jnp.where(rlive[0][:, None, None], gsum, 0.0)[None, None]
    left = pl.BlockSpec((64, BLK), lambda i: (0, i))
    grad_a = pl.pallas_call(
        kernel_add,
        grid=(CA // BLK,),
        in_specs=[left, left],
        out_specs=left,
        out_shape=jax.ShapeDtypeStruct((64, K), f32),
        compiler_params=params(8),
        name="add_a",
    )(ga_a, shift(ga_a, "c", 1))
    grad_a = pl.pallas_call(
        kernel_add_to,
        grid=(CB // BLK,),
        in_specs=[pl.BlockSpec(memory_space=pl.ANY), left, left],
        out_specs=pl.BlockSpec((64, BLK), lambda i: (0, i + CA // BLK)),
        out_shape=jax.ShapeDtypeStruct((64, K), f32),
        input_output_aliases={0: 0},
        compiler_params=params(8),
        name="add_b",
    )(grad_a, ga_b, shift(ga_b, "c", 1)).T
    mixed, grad_b = pl.pallas_call(
        kernel_final,
        in_specs=[vm],
        out_specs=[vm, vm],
        out_shape=[jax.ShapeDtypeStruct((NZ, 2, 16, 128), bf), jax.ShapeDtypeStruct((64, 128), f32)],
        compiler_params=params(),
        name="final",
    )(got)
    return (mixed.reshape(256, 128), grad_a, grad_b, grad_blocks)


def solution(mesh):
    finer = Mesh(mesh.devices.reshape(4, 8, 2, 4), ("x", "z", "c", "y"))
    in_specs = (
        P(DP, "y"),
        P(DP, "y"),
        P(DP, None),
        P("y", DP),
        P("y", None),
        P(),
        P(DP, "y", None, None, None),
        P(None, "y", None),
        P(None, "y", None),
        P(None, "y"),
    )
    out_specs = (P("y", DP), P("y", None), P(None, DP), P(DP, "y", None, None, None))
    return jax.shard_map(shards, mesh=finer, in_specs=in_specs, out_specs=out_specs, check_vma=False)
```

time: 161 us -> 136 us (0.84)
  blocking collectives: 41 us -> 0 us
  matrix products: 40.9 us -> 1.67 us
  starting transfers between devices: 29 us -> 68.1 us
  Pallas kernels: 0 us -> 27.1 us
  between operations: 15.5 us -> 0.98 us
  waiting for transfers between devices: 17.4 us -> 31.6 us
  other arithmetic: 8 us -> 2.07 us
  local copies, waits for them, and re-layouts: 8.89 us -> 4.4 us
    ppermute x0 -> x35, starting transfers between devices: none -> 53.6 us  [shift(): return lax.ppermute(a, axis, [(i, (i + k) % n) for i in range(n)])]
    all_gather x3 -> x0, blocking collectives: 41 us -> none  [all_blocks(): blocks = lax.all_gather(blocks, axes[k])]
    dot_general x10 -> x2, matrix products: 40.9 us -> 1.67 us  [the longest x1 1.32 us: shards(): lax.dot_general(cot, b, (((1,), (1,)), ((), ())), preferred_element_type=...]
    pallas_call x0 -> x8, Pallas kernels: none -> 27.1 us  [the longest x1 7.79 us: shards(): pl.pallas_call(functools.partial(kernel_b, places_b, nb), grid_spec=pltpu...]
    ppermute x0 -> x35, waiting for transfers between devices: none -> 22.5 us  [shift(): return lax.ppermute(a, axis, [(i, (i + k) % n) for i in range(n)])]
    all_to_all x4 -> x2, starting transfers between devices: 28.9 us -> 14.5 us  [the longest x1 9.5 us: shards(): lax.all_to_all(cot.reshape(16, 32, 256), ('x', 'z'), split_axis=1, concat...]
    all_gather x1 -> x0, waiting for transfers between devices: 5.64 us -> none  [shards(): hidden_gathered = lax.all_gather(hidden_activation, DP, axis=0, tiled=True)]
    all_to_all x2 -> x0, other arithmetic: 2.89 us -> none  [sent_to_all(): lax.all_to_all(jnp.broadcast_to(array[None], (count, *array.shape)), axis...]
  transfers between devices with their start and end apart: 5 -> 37, of which waited for: 3 -> 11; matrix products, arithmetic and copies ran while one was open for 18% -> 5% of each run, Pallas kernels for 0% -> 18%
where the time goes in v1:
time: 136 us
  starting transfers between devices  68.1 us (50%)
  waiting for transfers between devices  31.6 us (23%)
  Pallas kernels  27.1 us (20%)
  local copies, waits for them, and re-layouts  4.4 us (3%)
  other arithmetic  2.07 us (2%)
  matrix products  1.67 us (1%)
    ppermute x35, starting transfers between devices, shift(): return lax.ppermute(a, axis, [(i, (i + k) % n) for i in range(n)])  53.6 us
    ppermute x35, waiting for transfers between devices, shift(): return lax.ppermute(a, axis, [(i, (i + k) % n) for i in range(n)])  22.5 us
    all_to_all x1, starting transfers between devices, shards(): lax.all_to_all(cot.reshape(16, 32, 256), ('x', 'z'), split_axis=1, concat...  9.5 us
    all_to_all x1, waiting for transfers between devices, shards(): got = lax.all_to_all(send, ('c', 'y'), 0, 0, tiled=True)  9.06 us
    pallas_call x1, Pallas kernels, shards(): pl.pallas_call(functools.partial(kernel_b, places_b, nb), grid_spec=pltpu...  7.79 us
    pallas_call x1, Pallas kernels, shards(): pl.pallas_call(functools.partial(kernel_a, places_a, na), grid_spec=pltpu...  7.67 us
    pallas_call x1, Pallas kernels, shards(): pl.pallas_call(kernel_prep, grid_spec=pltpu.PrefetchScalarGridSpec(num_sc...  6.75 us
    all_to_all x1, starting transfers between devices, shards(): got = lax.all_to_all(send, ('c', 'y'), 0, 0, tiled=True)  4.97 us
  transfers between devices with their start and end apart: 37, of which 11 were waited for; matrix products, arithmetic and copies ran while one was open for 5% of the time, Pallas kernels for 18%

profile of v1, /device:TPU:1, one launch (start us, length us, event | category | flops | bytes accessed | tf_op | source)
XLA Modules:
  0.0 135.9 jit_solution(2089234461781169205)
XLA Ops:
  0.7 3.3 %collective-permute-start.13 = (bf16[7168,128]{1,0:T(8,128)(2,1)}, bf16[7168,128]{1,0:T(8,128)(2,1)}, u32[]{:S(2)}, u32[]{:S(2)}) collective-permute-start(bf16[7168,128]{1,0:T(8,128)(2,1)} %w_ref.1), channel_id=1, source_target_pairs={{0,4},{4,0},{1,5},{5,1},{2,6},{6,2},{3,7},{7,3},{8,12},{12,8},{9,1... | collective-permute-start | bytes 5505032 | tf_op jit(solution)/shard_map/ppermute | solution.py:25
  3.9 1.2 fusion.4
  5.2 0.1 collective-permute-start
  5.3 1.3 convolution_convert_fusion.1
  6.6 0.3 convolution_convert_fusion
  7.0 0.1 concatenate.7.refs_0_
  7.1 1.1 collective-permute-start.15
  8.2 4.0 %collective-permute-start.1 = (bf16[16,3584]{1,0:T(8,128)(2,1)S(1)}, bf16[16,3584]{1,0:T(8,128)(2,1)S(1)}, u32[]{:S(2)}, u32[]{:S(2)}) collective-permute-start(bf16[16,3584]{1,0:T(8,128)(2,1)S(1)} %get-tuple-element.35.refs_0_), channel_id=1, source_target_pairs={{0,56},{8,0},{16,8},{24,16},{32,24},{40,32},{48,40},{56,48},{1,57}... | collective-permute-start | bytes 344072 | tf_op jit(solution)/shard_map/ppermute | solution.py:25
  12.2 1.5 %collective-permute-start.16 = (bf16[16,3712]{1,0:T(8,128)(2,1)S(1)}, bf16[16,3712]{1,0:T(8,128)(2,1)S(1)}, u32[]{:S(2)}, u32[]{:S(2)}) collective-permute-start(bf16[16,3712]{1,0:T(8,128)(2,1)S(1)} %concatenate.7.refs_0_), channel_id=1, source_target_pairs={{0,192},{64,0},{128,64},{192,128},{1,193},{65,1},{129,65},{193,129... | collective-permute-start | bytes 356360 | tf_op jit(solution)/shard_map/ppermute | solution.py:25
  13.6 1.6 %collective-permute-start.17 = (bf16[16,3712]{1,0:T(8,128)(2,1)S(1)}, bf16[16,3712]{1,0:T(8,128)(2,1)S(1)}, u32[]{:S(2)}, u32[]{:S(2)}) collective-permute-start(bf16[16,3712]{1,0:T(8,128)(2,1)S(1)} %concatenate.7.refs_0_), channel_id=1, source_target_pairs={{0,128},{64,192},{128,0},{192,64},{1,129},{65,193},{129,1},{193,65... | collective-permute-start | bytes 356360 | tf_op jit(solution)/shard_map/ppermute | solution.py:25
  15.3 2.7 %collective-permute-start.3 = (bf16[16,3584]{1,0:T(8,128)(2,1)S(1)}, bf16[16,3584]{1,0:T(8,128)(2,1)S(1)}, u32[]{:S(2)}, u32[]{:S(2)}) collective-permute-start(bf16[16,3584]{1,0:T(8,128)(2,1)S(1)} %collective-permute-done.1.refs_2_), channel_id=1, source_target_pairs={{0,56},{8,0},{16,8},{24,16},{32,24},{40,32},{48,40},{56,48},{1,57}... | collective-permute-start | bytes 344072 | tf_op jit(solution)/shard_map/ppermute | solution.py:25
  18.0 0.9 collective-permute-done.17.refs_3_
  18.9 0.1 collective-permute-start.18
  19.0 1.4 %collective-permute-done.2.refs_3_ = bf16[16,3584]{1,0:T(8,128)(2,1)S(1)} collective-permute-done((bf16[16,3584]{1,0:T(8,128)(2,1)S(1)}, bf16[16,3584]{1,0:T(8,128)(2,1)S(1)}, u32[]{:S(2)}, u32[]{:S(2)}) %collective-permute-start.2) | collective-permute-done | bytes 114720 | tf_op jit(solution)/shard_map/ppermute | solution.py:25
  20.4 2.7 %collective-permute-start.5 = (bf16[16,3584]{1,0:T(8,128)(2,1)S(1)}, bf16[16,3584]{1,0:T(8,128)(2,1)S(1)}, u32[]{:S(2)}, u32[]{:S(2)}) collective-permute-start(bf16[16,3584]{1,0:T(8,128)(2,1)S(1)} %collective-permute-done.3.refs_4_), channel_id=1, source_target_pairs={{0,56},{8,0},{16,8},{24,16},{32,24},{40,32},{48,40},{56,48},{1,57}... | collective-permute-start | bytes 344072 | tf_op jit(solution)/shard_map/ppermute | solution.py:25
  23.1 2.6 %collective-permute-start.14 = (bf16[2,128,128]{2,1,0:T(8,128)(2,1)S(1)}, bf16[2,128,128]{2,1,0:T(8,128)(2,1)S(1)}, u32[]{:S(2)}, u32[]{:S(2)}) collective-permute-start(bf16[2,128,128]{2,1,0:T(8,128)(2,1)S(1)} %bitcast.32), channel_id=1, source_target_pairs={{0,4},{4,0},{1,5},{5,1},{2,6},{6,2},{3,7},{7,3},{8,12},{12,8},{9,1... | collective-permute-start | bytes 196616 | tf_op jit(solution)/shard_map/ppermute | solution.py:25
  25.7 0.9 collective-permute-done.14.spo_ref
  26.6 0.4 collective-permute-start.20
  27.0 0.9 collective-permute-done.4.refs_5_
  27.9 0.2 collective-permute-start.19
  28.1 2.5 %collective-permute-start.21 = (bf16[2,16,3712]{2,1,0:T(8,128)(2,1)S(1)}, bf16[2,16,3712]{2,1,0:T(8,128)(2,1)}, u32[]{:S(2)}, u32[]{:S(2)}) collective-permute-start(bf16[2,16,3712]{2,1,0:T(8,128)(2,1)S(1)} %get-tuple-element.20.refs_0_.refs_16_), channel_id=1, source_target_pairs={{0,56},{8,0},{16,8},{24,16},{32,24},{40,32},{48,40},{56,48},{1,57}... | collective-permute-start | bytes 712712 | tf_op jit(solution)/shard_map/ppermute | solution.py:25
  30.5 3.0 %collective-permute-done.20.refs_4_.refs_20_ = bf16[2,16,3712]{2,1,0:T(8,128)(2,1)S(1)} collective-permute-done((bf16[2,16,3712]{2,1,0:T(8,128)(2,1)S(1)}, bf16[2,16,3712]{2,1,0:T(8,128)(2,1)S(1)}, u32[]{:S(2)}, u32[]{:S(2)}) %collective-permute-start.20) | collective-permute-done | bytes 237600 | tf_op jit(solution)/shard_map/ppermute | solution.py:25
  33.6 0.7 collective-permute-start.6
  34.2 2.0 %collective-permute-start.24 = (bf16[2,16,3712]{2,1,0:T(8,128)(2,1)S(1)}, bf16[2,16,3712]{2,1,0:T(8,128)(2,1)}, u32[]{:S(2)}, u32[]{:S(2)}) collective-permute-start(bf16[2,16,3712]{2,1,0:T(8,128)(2,1)S(1)} %collective-permute-done.20.refs_4_.refs_20_), channel_id=1, source_target_pairs={{0,56},{8,0},{16,8},{24,16},{32,24},{40,32},{48,40},{56,48},{1,57}... | collective-permute-start | bytes 712712 | tf_op jit(solution)/shard_map/ppermute | solution.py:25
  36.3 2.5 %collective-permute-done.21.refs_5_.refs_21_ = bf16[2,16,3712]{2,1,0:T(8,128)(2,1)} collective-permute-done((bf16[2,16,3712]{2,1,0:T(8,128)(2,1)S(1)}, bf16[2,16,3712]{2,1,0:T(8,128)(2,1)}, u32[]{:S(2)}, u32[]{:S(2)}) %collective-permute-start.21) | collective-permute-done | bytes 237600 | tf_op jit(solution)/shard_map/ppermute | solution.py:25
  38.8 0.3 collective-permute-start.23
  39.1 2.3 %collective-permute-done.6.refs_7_ = bf16[16,3584]{1,0:T(8,128)(2,1)S(1)} collective-permute-done((bf16[16,3584]{1,0:T(8,128)(2,1)S(1)}, bf16[16,3584]{1,0:T(8,128)(2,1)S(1)}, u32[]{:S(2)}, u32[]{:S(2)}) %collective-permute-start.6) | collective-permute-done | bytes 114720 | tf_op jit(solution)/shard_map/ppermute | solution.py:25
  41.4 0.1 collective-permute-start.25
  41.5 1.4 %collective-permute-start.26 = (bf16[2,16,3712]{2,1,0:T(8,128)(2,1)}, bf16[2,16,3712]{2,1,0:T(8,128)(2,1)}, u32[]{:S(2)}, u32[]{:S(2)}) collective-permute-start(bf16[2,16,3712]{2,1,0:T(8,128)(2,1)} %collective-permute-done.22.refs_6_.refs_22_), channel_id=1, source_target_pairs={{0,8},{8,16},{16,24},{24,32},{32,40},{40,48},{48,56},{56,0},{1,9},... | collective-permute-start | bytes 712712 | tf_op jit(solution)/shard_map/ppermute | solution.py:25
  42.9 0.9 copy.18
  43.7 9.5 %all-to-all-start = ((bf16[1,16,32,256]{3,1,0,2:T(8,128)(2,1)}), bf16[1,16,32,256]{3,1,0,2:T(8,128)(2,1)}, u32[]{:S(2)}, u32[]{:S(2)}) async-start(bf16[1,16,32,256]{3,1,0,2:T(8,128)(2,1)} %copy.18), calls=%async_computation | async-start | bytes 524288 | tf_op jit(solution)/shard_map/all_to_all | solution.py:222
  53.3 2.4 %collective-permute-start.28 = (bf16[2,16,3712]{2,1,0:T(8,128)(2,1)}, bf16[2,16,3712]{2,1,0:T(8,128)(2,1)}, u32[]{:S(2)}, u32[]{:S(2)}) collective-permute-start(bf16[2,16,3712]{2,1,0:T(8,128)(2,1)} %collective-permute-done.24.refs_8_.refs_24_), channel_id=1, source_target_pairs={{0,56},{8,0},{16,8},{24,16},{32,24},{40,32},{48,40},{56,48},{1,57}... | collective-permute-start | bytes 712712 | tf_op jit(solution)/shard_map/ppermute | solution.py:25
  55.7 0.1 fusion.5
  55.9 1.3 collective-permute-start.7
  57.2 1.5 %collective-permute-start.10 = (bf16[4,16,3584]{2,1,0:T(8,128)(2,1)S(1)}, bf16[4,16,3584]{2,1,0:T(8,128)(2,1)}, u32[]{:S(2)}, u32[]{:S(2)}) collective-permute-start(bf16[4,16,3584]{2,1,0:T(8,128)(2,1)S(1)} %get-tuple-element.19.refs_1_), channel_id=1, source_target_pairs={{0,192},{64,0},{128,64},{192,128},{1,193},{65,1},{129,65},{193,129... | collective-permute-start | bytes 1376264 | tf_op jit(solution)/shard_map/ppermute | solution.py:25
  58.7 2.1 %collective-permute-done.28.refs_12_.refs_28_ = bf16[2,16,3712]{2,1,0:T(8,128)(2,1)} collective-permute-done((bf16[2,16,3712]{2,1,0:T(8,128)(2,1)}, bf16[2,16,3712]{2,1,0:T(8,128)(2,1)}, u32[]{:S(2)}, u32[]{:S(2)}) %collective-permute-start.28) | collective-permute-done | bytes 237600 | tf_op jit(solution)/shard_map/ppermute | solution.py:25
  60.9 2.0 %collective-permute-start.29 = (bf16[2,16,3712]{2,1,0:T(8,128)(2,1)}, bf16[2,16,3712]{2,1,0:T(8,128)(2,1)S(1)}, u32[]{:S(2)}, u32[]{:S(2)}) collective-permute-start(bf16[2,16,3712]{2,1,0:T(8,128)(2,1)} %collective-permute-done.25.refs_9_.refs_25_), channel_id=1, source_target_pairs={{0,56},{8,0},{16,8},{24,16},{32,24},{40,32},{48,40},{56,48},{1,57}... | collective-permute-start | bytes 712712 | tf_op jit(solution)/shard_map/ppermute | solution.py:25
  62.9 0.1 constant_dynamic-slice_fusion.2
  63.0 0.1 copy.17
  63.1 7.2 %collective-permute-done.29.refs_13_.refs_29_ = bf16[2,16,3712]{2,1,0:T(8,128)(2,1)S(1)} collective-permute-done((bf16[2,16,3712]{2,1,0:T(8,128)(2,1)}, bf16[2,16,3712]{2,1,0:T(8,128)(2,1)S(1)}, u32[]{:S(2)}, u32[]{:S(2)}) %collective-permute-start.29) | collective-permute-done | bytes 237600 | tf_op jit(solution)/shard_map/ppermute | solution.py:25
  70.3 1.2 collective-permute-start.8
  71.5 1.5 %collective-permute-start.9 = (bf16[4,16,3584]{2,1,0:T(8,128)(2,1)S(1)}, bf16[4,16,3584]{2,1,0:T(8,128)(2,1)}, u32[]{:S(2)}, u32[]{:S(2)}) collective-permute-start(bf16[4,16,3584]{2,1,0:T(8,128)(2,1)S(1)} %get-tuple-element.18.refs_0_), channel_id=1, source_target_pairs={{0,192},{64,0},{128,64},{192,128},{1,193},{65,1},{129,65},{193,129... | collective-permute-start | bytes 1376264 | tf_op jit(solution)/shard_map/ppermute | solution.py:25
  73.0 2.4 %collective-permute-start.31 = (bf16[2,16,3712]{2,1,0:T(8,128)(2,1)}, bf16[2,16,3712]{2,1,0:T(8,128)(2,1)S(1)}, u32[]{:S(2)}, u32[]{:S(2)}) collective-permute-start(bf16[2,16,3712]{2,1,0:T(8,128)(2,1)} %collective-permute-done.28.refs_12_.refs_28_), channel_id=1, source_target_pairs={{0,56},{8,0},{16,8},{24,16},{32,24},{40,32},{48,40},{56,48},{1,57}... | collective-permute-start | bytes 712712 | tf_op jit(solution)/shard_map/ppermute | solution.py:25
  75.4 0.4 collective-permute-start.11
  75.9 2.2 %collective-permute-start.12 = (bf16[4,16,3584]{2,1,0:T(8,128)(2,1)}, bf16[4,16,3584]{2,1,0:T(8,128)(2,1)}, u32[]{:S(2)}, u32[]{:S(2)}) collective-permute-start(bf16[4,16,3584]{2,1,0:T(8,128)(2,1)} %collective-permute-done.10.refs_5_), channel_id=1, source_target_pairs={{0,192},{64,0},{128,64},{192,128},{1,193},{65,1},{129,65},{193,129... | collective-permute-start | bytes 1376264 | tf_op jit(solution)/shard_map/ppermute | solution.py:25
  78.2 0.1 reshape.30
  78.3 0.1 reshape.25
  78.4 0.6 concatenate.6.s_ref
  79.0 0.6 constant_dynamic-slice_fusion.b_ref
  79.6 6.8 %prep.1.refs_32_.refs_8_ = bf16[7168,256]{1,0:T(8,128)(2,1)} custom-call(s32[11]{0:T(128)} %concatenate.6.s_ref, bf16[7168,128]{1,0:T(8,128)(2,1)} %w_ref.1, bf16[7168,128]{1,0:T(8,128)(2,1)} %collective-permute-done.13.wo_ref, bf16[64,7168]{1,0:T(8,128)(2,1)} %bitcast.28, bf16[64,256]{1,0:T(8,128)(2,1)} %constant_dynamic-slice_fusion.b_ref, ...), custom_call_target="tpu_custom_call" | custom-call | flops 268435456 | bytes 8388608 | tf_op jit(solution)/shard_map/prep/pallas_call | solution.py:233
  86.4 0.7 copy-done.13
  87.1 7.7 %colour_a.1 = (f32[512,256]{1,0:T(8,128)}, f32[64,3584]{1,0:T(8,128)}, bf16[128,512]{1,0:T(8,128)(2,1)}, bf16[512,128]{1,0:T(8,128)(2,1)}, f32[4,128,128]{2,1,0:T(8,128)}) custom-call(s32[11]{0:T(128)} %concatenate.6.s_ref, bf16[2,16,3712]{2,1,0:T(8,128)(2,1)} %copy-done.1, bf16[2,16,3712]{2,1,0:T(8,128)(2,1)} %copy-done.2, bf16[2,16,3712]{2,1,0:T(8,128)(2,1)} %copy-done.9, ...), custom_call_target="tpu_custom_call" | custom-call | flops 1409286144 | bytes 12582912 | tf_op jit(solution)/shard_map/colour_a/pallas_call | solution.py:253
  94.8 11.2 %collective-permute-start.32 = (f32[64,3584]{1,0:T(8,128)}, f32[64,3584]{1,0:T(8,128)}, u32[]{:S(2)}, u32[]{:S(2)}) collective-permute-start(f32[64,3584]{1,0:T(8,128)} %get-tuple-element.28.x_ref), channel_id=1, source_target_pairs={{0,4},{4,0},{1,5},{5,1},{2,6},{6,2},{3,7},{7,3},{8,12},{12,8},{9,1... | collective-permute-start | bytes 2752520 | tf_op jit(solution)/shard_map/ppermute | solution.py:25
  106.0 7.8 %colour_b.1 = (f32[8,192,128]{2,1,0:T(8,128)}, f32[64,3584]{1,0:T(8,128)}, f32[4,128,128]{2,1,0:T(8,128)}) custom-call(s32[11]{0:T(128)} %concatenate.6.s_ref, bf16[4,16,3584]{2,1,0:T(8,128)(2,1)} %copy-done.5, bf16[4,16,3584]{2,1,0:T(8,128)(2,1)} %copy-done.6, bf16[4,16,3584]{2,1,0:T(8,128)(2,1)} %copy-done.14, ...), custom_call_target="tpu_custom_call" | custom-call | flops 1409286144 | bytes 12582912 | tf_op jit(solution)/shard_map/colour_b/pallas_call | solution.py:275
  113.8 0.1 collective-permute-start.33
  114.0 5.0 %all-to-all-start.1 = ((f32[8,192,128]{2,1,0:T(8,128)}), f32[8,192,128]{2,1,0:T(8,128)S(1)}, u32[]{:S(2)}, u32[]{:S(2)}) async-start(f32[8,192,128]{2,1,0:T(8,128)} %get-tuple-element.26), calls=%async_computation.1 | async-start | bytes 1572864 | tf_op jit(solution)/shard_map/all_to_all | solution.py:302
  118.9 0.9 slice.19
  119.8 0.1 collective-permute-start.34
  120.0 1.3 collective-permute-done.34
  121.3 0.7 select_bitcast_fusion
  122.0 9.1 %all-to-all-done.1.got_ref = f32[8,192,128]{2,1,0:T(8,128)S(1)} async-done(((f32[8,192,128]{2,1,0:T(8,128)}), f32[8,192,128]{2,1,0:T(8,128)S(1)}, u32[]{:S(2)}, u32[]{:S(2)}) %all-to-all-start.1) | async-done | bytes 786464 | tf_op jit(solution)/shard_map/all_to_all | solution.py:302
  131.1 0.7 final.1
  131.8 2.1 %add_a.1._ = f32[64,7168]{1,0:T(8,128)} custom-call(f32[64,3584]{1,0:T(8,128)S(1)} %copy-done.3, f32[64,3584]{1,0:T(8,128)} %collective-permute-done.32.y_ref), custom_call_target="tpu_custom_call" | custom-call | tf_op jit(solution)/shard_map/add_a/pallas_call | solution.py:306
  133.9 2.0 %add_b.1 = f32[64,7168]{1,0:T(8,128)} custom-call(f32[64,7168]{1,0:T(8,128)} %add_a.1._, f32[64,3584]{1,0:T(8,128)S(1)} %copy-done.4, f32[64,3584]{1,0:T(8,128)} %collective-permute-done.33.y_ref), custom_call_target="tpu_custom_call", output_to_operand_aliasing={{}: (0, {})} | custom-call | tf_op jit(solution)/shard_map/add_b/pallas_call | solution.py:315
  (80 shorter events, 0.5 us)
Async XLA Ops:
  0.6 4.6 %copy-start = (bf16[64,8192]{1,0:T(8,128)(2,1)S(1)}, bf16[64,8192]{1,0:T(8,128)(2,1)}, u32[]{:S(2)}) copy-start(bf16[64,8192]{1,0:T(8,128)(2,1)} %param.15) | copy-start | bytes 3145732
  0.6 6.0 %copy-start.7 = (bf16[7168,64]{0,1:T(8,128)(2,1)S(1)}, bf16[7168,64]{0,1:T(8,128)(2,1)}, u32[]{:S(2)}) copy-start(bf16[7168,64]{0,1:T(8,128)(2,1)} %param.14) | copy-start | bytes 2752516
  0.7 75.2 %collective-permute-start.13 = (bf16[7168,128]{1,0:T(8,128)(2,1)}, bf16[7168,128]{1,0:T(8,128)(2,1)}, u32[]{:S(2)}, u32[]{:S(2)}) collective-permute-start(bf16[7168,128]{1,0:T(8,128)(2,1)} %w_ref.1), channel_id=1, source_target_pairs={{0,4},{4,0},{1,5},{5,1},{2,6},{6,2},{3,7},{7,3},{8,12},{12,8},{9,1... | collective-permute-start | bytes 5505032 | tf_op jit(solution)/shard_map/ppermute | solution.py:25
  5.1 18.0 %copy-start.16 = (bf16[1,1,2,128,128]{4,3,2,1,0:T(8,128)(2,1)S(1)}, bf16[1,1,2,128,128]{4,3,2,1,0:T(8,128)(2,1)}, u32[]{:S(2)}) copy-start(bf16[1,1,2,128,128]{4,3,2,1,0:T(8,128)(2,1)} %param.16) | copy-start | bytes 196612
  5.1 37.7 %copy-start.8 = (bf16[16,8192]{1,0:T(8,128)(2,1)S(1)}, bf16[16,8192]{1,0:T(8,128)(2,1)}, u32[]{:S(2)}) copy-start(bf16[16,8192]{1,0:T(8,128)(2,1)} %param.12) | copy-start | bytes 786436
  5.2 8.5 %collective-permute-start = (bf16[16,3584]{1,0:T(8,128)(2,1)S(1)}, bf16[16,3584]{1,0:T(8,128)(2,1)S(1)}, u32[]{:S(2)}, u32[]{:S(2)}) collective-permute-start(bf16[16,3584]{1,0:T(8,128)(2,1)S(1)} %get-tuple-element.35.refs_0_), channel_id=1, source_target_pairs={{0,8},{8,16},{16,24},{24,32},{32,40},{40,48},{48,56},{56,0},{1,9},... | collective-permute-start | bytes 344072 | tf_op jit(solution)/shard_map/ppermute | solution.py:25
  6.6 49.1 %copy-start.19 = (s32[64,1]{0,1:T(1,128)S(1)}, s32[64,1]{0,1:T(1,128)}, u32[]{:S(2)}) copy-start(s32[64,1]{0,1:T(1,128)} %param.18) | copy-start | bytes 772
  7.0 55.9 %copy-start.18 = (s32[64,1,2]{0,2,1:T(2,128)S(1)}, s32[64,1,2]{0,2,1:T(2,128)}, u32[]{:S(2)}) copy-start(s32[64,1,2]{0,2,1:T(2,128)} %param.17) | copy-start | bytes 1540
  7.1 8.2 %collective-permute-start.15 = (bf16[16,3712]{1,0:T(8,128)(2,1)S(1)}, bf16[16,3712]{1,0:T(8,128)(2,1)S(1)}, u32[]{:S(2)}, u32[]{:S(2)}) collective-permute-start(bf16[16,3712]{1,0:T(8,128)(2,1)S(1)} %concatenate.7.refs_0_), channel_id=1, source_target_pairs={{0,64},{64,128},{128,192},{192,0},{1,65},{65,129},{129,193},{193,1... | collective-permute-start | bytes 356360 | tf_op jit(solution)/shard_map/ppermute | solution.py:25
  8.2 7.0 %collective-permute-start.1 = (bf16[16,3584]{1,0:T(8,128)(2,1)S(1)}, bf16[16,3584]{1,0:T(8,128)(2,1)S(1)}, u32[]{:S(2)}, u32[]{:S(2)}) collective-permute-start(bf16[16,3584]{1,0:T(8,128)(2,1)S(1)} %get-tuple-element.35.refs_0_), channel_id=1, source_target_pairs={{0,56},{8,0},{16,8},{24,16},{32,24},{40,32},{48,40},{56,48},{1,57}... | collective-permute-start | bytes 344072 | tf_op jit(solution)/shard_map/ppermute | solution.py:25
  12.2 5.8 %collective-permute-start.16 = (bf16[16,3712]{1,0:T(8,128)(2,1)S(1)}, bf16[16,3712]{1,0:T(8,128)(2,1)S(1)}, u32[]{:S(2)}, u32[]{:S(2)}) collective-permute-start(bf16[16,3712]{1,0:T(8,128)(2,1)S(1)} %concatenate.7.refs_0_), channel_id=1, source_target_pairs={{0,192},{64,0},{128,64},{192,128},{1,193},{65,1},{129,65},{193,129... | collective-permute-start | bytes 356360 | tf_op jit(solution)/shard_map/ppermute | solution.py:25
  13.6 5.2 %collective-permute-start.17 = (bf16[16,3712]{1,0:T(8,128)(2,1)S(1)}, bf16[16,3712]{1,0:T(8,128)(2,1)S(1)}, u32[]{:S(2)}, u32[]{:S(2)}) collective-permute-start(bf16[16,3712]{1,0:T(8,128)(2,1)S(1)} %concatenate.7.refs_0_), channel_id=1, source_target_pairs={{0,128},{64,192},{128,0},{192,64},{1,129},{65,193},{129,1},{193,65... | collective-permute-start | bytes 356360 | tf_op jit(solution)/shard_map/ppermute | solution.py:25
  15.3 5.1 %collective-permute-start.2 = (bf16[16,3584]{1,0:T(8,128)(2,1)S(1)}, bf16[16,3584]{1,0:T(8,128)(2,1)S(1)}, u32[]{:S(2)}, u32[]{:S(2)}) collective-permute-start(bf16[16,3584]{1,0:T(8,128)(2,1)S(1)} %collective-permute-done.refs_1_), channel_id=1, source_target_pairs={{0,8},{8,16},{16,24},{24,32},{32,40},{40,48},{48,56},{56,0},{1,9},... | collective-permute-start | bytes 344072 | tf_op jit(solution)/shard_map/ppermute | solution.py:25
  15.3 5.1 %collective-permute-start.3 = (bf16[16,3584]{1,0:T(8,128)(2,1)S(1)}, bf16[16,3584]{1,0:T(8,128)(2,1)S(1)}, u32[]{:S(2)}, u32[]{:S(2)}) collective-permute-start(bf16[16,3584]{1,0:T(8,128)(2,1)S(1)} %collective-permute-done.1.refs_2_), channel_id=1, source_target_pairs={{0,56},{8,0},{16,8},{24,16},{32,24},{40,32},{48,40},{56,48},{1,57}... | collective-permute-start | bytes 344072 | tf_op jit(solution)/shard_map/ppermute | solution.py:25
  18.9 67.5 %copy-start.1 = (bf16[2,16,3712]{2,1,0:T(8,128)(2,1)}, bf16[2,16,3712]{2,1,0:T(8,128)(2,1)S(1)}, u32[]{:S(2)}) copy-start(bf16[2,16,3712]{2,1,0:T(8,128)(2,1)S(1)} %get-tuple-element.20.refs_0_.refs_16_) | copy-start | bytes 712708
  18.9 67.4 %copy-start.2 = (bf16[2,16,3712]{2,1,0:T(8,128)(2,1)}, bf16[2,16,3712]{2,1,0:T(8,128)(2,1)S(1)}, u32[]{:S(2)}) copy-start(bf16[2,16,3712]{2,1,0:T(8,128)(2,1)S(1)} %get-tuple-element.21.refs_1_.refs_17_) | copy-start | bytes 712708
  18.9 11.6 %collective-permute-start.18 = (bf16[2,16,3712]{2,1,0:T(8,128)(2,1)S(1)}, bf16[2,16,3712]{2,1,0:T(8,128)(2,1)S(1)}, u32[]{:S(2)}, u32[]{:S(2)}) collective-permute-start(bf16[2,16,3712]{2,1,0:T(8,128)(2,1)S(1)} %get-tuple-element.20.refs_0_.refs_16_), channel_id=1, source_target_pairs={{0,8},{8,16},{16,24},{24,32},{32,40},{40,48},{48,56},{56,0},{1,9},... | collective-permute-start | bytes 712712 | tf_op jit(solution)/shard_map/ppermute | solution.py:25
  20.4 7.4 %collective-permute-start.4 = (bf16[16,3584]{1,0:T(8,128)(2,1)S(1)}, bf16[16,3584]{1,0:T(8,128)(2,1)S(1)}, u32[]{:S(2)}, u32[]{:S(2)}) collective-permute-start(bf16[16,3584]{1,0:T(8,128)(2,1)S(1)} %collective-permute-done.2.refs_3_), channel_id=1, source_target_pairs={{0,8},{8,16},{16,24},{24,32},{32,40},{40,48},{48,56},{56,0},{1,9},... | collective-permute-start | bytes 344072 | tf_op jit(solution)/shard_map/ppermute | solution.py:25
  20.4 7.6 %collective-permute-start.5 = (bf16[16,3584]{1,0:T(8,128)(2,1)S(1)}, bf16[16,3584]{1,0:T(8,128)(2,1)S(1)}, u32[]{:S(2)}, u32[]{:S(2)}) collective-permute-start(bf16[16,3584]{1,0:T(8,128)(2,1)S(1)} %collective-permute-done.3.refs_4_), channel_id=1, source_target_pairs={{0,56},{8,0},{16,8},{24,16},{32,24},{40,32},{48,40},{56,48},{1,57}... | collective-permute-start | bytes 344072 | tf_op jit(solution)/shard_map/ppermute | solution.py:25
  23.1 3.5 %collective-permute-start.14 = (bf16[2,128,128]{2,1,0:T(8,128)(2,1)S(1)}, bf16[2,128,128]{2,1,0:T(8,128)(2,1)S(1)}, u32[]{:S(2)}, u32[]{:S(2)}) collective-permute-start(bf16[2,128,128]{2,1,0:T(8,128)(2,1)S(1)} %bitcast.32), channel_id=1, source_target_pairs={{0,4},{4,0},{1,5},{5,1},{2,6},{6,2},{3,7},{7,3},{8,12},{12,8},{9,1... | collective-permute-start | bytes 196616 | tf_op jit(solution)/shard_map/ppermute | solution.py:25
  26.6 16.2 %copy-start.17 = (bf16[2,128,128]{2,1,0:T(8,128)(2,1)}, bf16[2,128,128]{2,1,0:T(8,128)(2,1)S(1)}, u32[]{:S(2)}) copy-start(bf16[2,128,128]{2,1,0:T(8,128)(2,1)S(1)} %collective-permute-done.14.spo_ref) | copy-start | bytes 196612
  26.6 7.0 %collective-permute-start.20 = (bf16[2,16,3712]{2,1,0:T(8,128)(2,1)S(1)}, bf16[2,16,3712]{2,1,0:T(8,128)(2,1)S(1)}, u32[]{:S(2)}, u32[]{:S(2)}) collective-permute-start(bf16[2,16,3712]{2,1,0:T(8,128)(2,1)S(1)} %get-tuple-element.21.refs_1_.refs_17_), channel_id=1, source_target_pairs={{0,56},{8,0},{16,8},{24,16},{32,24},{40,32},{48,40},{56,48},{1,57}... | collective-permute-start | bytes 712712 | tf_op jit(solution)/shard_map/ppermute | solution.py:25
  27.9 6.4 %collective-permute-start.19 = (bf16[2,16,3712]{2,1,0:T(8,128)(2,1)S(1)}, bf16[2,16,3712]{2,1,0:T(8,128)(2,1)}, u32[]{:S(2)}, u32[]{:S(2)}) collective-permute-start(bf16[2,16,3712]{2,1,0:T(8,128)(2,1)S(1)} %get-tuple-element.21.refs_1_.refs_17_), channel_id=1, source_target_pairs={{0,8},{8,16},{16,24},{24,32},{32,40},{40,48},{48,56},{56,0},{1,9},... | collective-permute-start | bytes 712712 | tf_op jit(solution)/shard_map/ppermute | solution.py:25
  28.1 10.7 %collective-permute-start.21 = (bf16[2,16,3712]{2,1,0:T(8,128)(2,1)S(1)}, bf16[2,16,3712]{2,1,0:T(8,128)(2,1)}, u32[]{:S(2)}, u32[]{:S(2)}) collective-permute-start(bf16[2,16,3712]{2,1,0:T(8,128)(2,1)S(1)} %get-tuple-element.20.refs_0_.refs_16_), channel_id=1, source_target_pairs={{0,56},{8,0},{16,8},{24,16},{32,24},{40,32},{48,40},{56,48},{1,57}... | collective-permute-start | bytes 712712 | tf_op jit(solution)/shard_map/ppermute | solution.py:25
  30.5 12.3 %copy-start.9 = (bf16[2,16,3712]{2,1,0:T(8,128)(2,1)}, bf16[2,16,3712]{2,1,0:T(8,128)(2,1)S(1)}, u32[]{:S(2)}) copy-start(bf16[2,16,3712]{2,1,0:T(8,128)(2,1)S(1)} %collective-permute-done.18.refs_2_.refs_18_) | copy-start | bytes 712708
  30.5 10.9 %collective-permute-start.22 = (bf16[2,16,3712]{2,1,0:T(8,128)(2,1)S(1)}, bf16[2,16,3712]{2,1,0:T(8,128)(2,1)}, u32[]{:S(2)}, u32[]{:S(2)}) collective-permute-start(bf16[2,16,3712]{2,1,0:T(8,128)(2,1)S(1)} %collective-permute-done.18.refs_2_.refs_18_), channel_id=1, source_target_pairs={{0,8},{8,16},{16,24},{24,32},{32,40},{40,48},{48,56},{56,0},{1,9},... | collective-permute-start | bytes 712712 | tf_op jit(solution)/shard_map/ppermute | solution.py:25
  33.6 22.1 %copy-start.10 = (bf16[2,16,3712]{2,1,0:T(8,128)(2,1)}, bf16[2,16,3712]{2,1,0:T(8,128)(2,1)S(1)}, u32[]{:S(2)}) copy-start(bf16[2,16,3712]{2,1,0:T(8,128)(2,1)S(1)} %collective-permute-done.20.refs_4_.refs_20_) | copy-start | bytes 712708
  33.6 7.8 %collective-permute-start.6 = (bf16[16,3584]{1,0:T(8,128)(2,1)S(1)}, bf16[16,3584]{1,0:T(8,128)(2,1)S(1)}, u32[]{:S(2)}, u32[]{:S(2)}) collective-permute-start(bf16[16,3584]{1,0:T(8,128)(2,1)S(1)} %collective-permute-done.4.refs_5_), channel_id=1, source_target_pairs={{0,8},{8,16},{16,24},{24,32},{32,40},{40,48},{48,56},{56,0},{1,9},... | collective-permute-start | bytes 344072 | tf_op jit(solution)/shard_map/ppermute | solution.py:25
  34.2 19.0 %collective-permute-start.24 = (bf16[2,16,3712]{2,1,0:T(8,128)(2,1)S(1)}, bf16[2,16,3712]{2,1,0:T(8,128)(2,1)}, u32[]{:S(2)}, u32[]{:S(2)}) collective-permute-start(bf16[2,16,3712]{2,1,0:T(8,128)(2,1)S(1)} %collective-permute-done.20.refs_4_.refs_20_), channel_id=1, source_target_pairs={{0,56},{8,0},{16,8},{24,16},{32,24},{40,32},{48,40},{56,48},{1,57}... | collective-permute-start | bytes 712712 | tf_op jit(solution)/shard_map/ppermute | solution.py:25
  38.8 16.9 %collective-permute-start.23 = (bf16[2,16,3712]{2,1,0:T(8,128)(2,1)}, bf16[2,16,3712]{2,1,0:T(8,128)(2,1)}, u32[]{:S(2)}, u32[]{:S(2)}) collective-permute-start(bf16[2,16,3712]{2,1,0:T(8,128)(2,1)} %collective-permute-done.19.refs_3_.refs_19_), channel_id=1, source_target_pairs={{0,8},{8,16},{16,24},{24,32},{32,40},{40,48},{48,56},{56,0},{1,9},... | collective-permute-start | bytes 712712 | tf_op jit(solution)/shard_map/ppermute | solution.py:25
  41.4 14.5 %collective-permute-start.25 = (bf16[2,16,3712]{2,1,0:T(8,128)(2,1)}, bf16[2,16,3712]{2,1,0:T(8,128)(2,1)}, u32[]{:S(2)}, u32[]{:S(2)}) collective-permute-start(bf16[2,16,3712]{2,1,0:T(8,128)(2,1)} %collective-permute-done.21.refs_5_.refs_21_), channel_id=1, source_target_pairs={{0,56},{8,0},{16,8},{24,16},{32,24},{40,32},{48,40},{56,48},{1,57}... | collective-permute-start | bytes 712712 | tf_op jit(solution)/shard_map/ppermute | solution.py:25
  41.5 15.7 %collective-permute-start.26 = (bf16[2,16,3712]{2,1,0:T(8,128)(2,1)}, bf16[2,16,3712]{2,1,0:T(8,128)(2,1)}, u32[]{:S(2)}, u32[]{:S(2)}) collective-permute-start(bf16[2,16,3712]{2,1,0:T(8,128)(2,1)} %collective-permute-done.22.refs_6_.refs_22_), channel_id=1, source_target_pairs={{0,8},{8,16},{16,24},{24,32},{32,40},{40,48},{48,56},{56,0},{1,9},... | collective-permute-start | bytes 712712 | tf_op jit(solution)/shard_map/ppermute | solution.py:25
  43.7 42.6 %all-to-all-start = ((bf16[1,16,32,256]{3,1,0,2:T(8,128)(2,1)}), bf16[1,16,32,256]{3,1,0,2:T(8,128)(2,1)}, u32[]{:S(2)}, u32[]{:S(2)}) async-start(bf16[1,16,32,256]{3,1,0,2:T(8,128)(2,1)} %copy.18), calls=%async_computation | async-start | bytes 524288 | tf_op jit(solution)/shard_map/all_to_all | solution.py:222
  53.3 7.6 %collective-permute-start.28 = (bf16[2,16,3712]{2,1,0:T(8,128)(2,1)}, bf16[2,16,3712]{2,1,0:T(8,128)(2,1)}, u32[]{:S(2)}, u32[]{:S(2)}) collective-permute-start(bf16[2,16,3712]{2,1,0:T(8,128)(2,1)} %collective-permute-done.24.refs_8_.refs_24_), channel_id=1, source_target_pairs={{0,56},{8,0},{16,8},{24,16},{32,24},{40,32},{48,40},{56,48},{1,57}... | collective-permute-start | bytes 712712 | tf_op jit(solution)/shard_map/ppermute | solution.py:25
  55.7 7.2 %collective-permute-start.27 = (bf16[2,16,3712]{2,1,0:T(8,128)(2,1)}, bf16[2,16,3712]{2,1,0:T(8,128)(2,1)}, u32[]{:S(2)}, u32[]{:S(2)}) collective-permute-start(bf16[2,16,3712]{2,1,0:T(8,128)(2,1)} %collective-permute-done.23.refs_7_.refs_23_), channel_id=1, source_target_pairs={{0,8},{8,16},{16,24},{24,32},{32,40},{40,48},{48,56},{56,0},{1,9},... | collective-permute-start | bytes 712712 | tf_op jit(solution)/shard_map/ppermute | solution.py:25
  55.9 30.5 %copy-start.5 = (bf16[4,16,3584]{2,1,0:T(8,128)(2,1)}, bf16[4,16,3584]{2,1,0:T(8,128)(2,1)S(1)}, u32[]{:S(2)}) copy-start(bf16[4,16,3584]{2,1,0:T(8,128)(2,1)S(1)} %get-tuple-element.18.refs_0_) | copy-start | bytes 1376260
  55.9 30.5 %copy-start.6 = (bf16[4,16,3584]{2,1,0:T(8,128)(2,1)}, bf16[4,16,3584]{2,1,0:T(8,128)(2,1)S(1)}, u32[]{:S(2)}) copy-start(bf16[4,16,3584]{2,1,0:T(8,128)(2,1)S(1)} %get-tuple-element.19.refs_1_) | copy-start | bytes 1376260
  55.9 15.6 %collective-permute-start.7 = (bf16[4,16,3584]{2,1,0:T(8,128)(2,1)S(1)}, bf16[4,16,3584]{2,1,0:T(8,128)(2,1)S(1)}, u32[]{:S(2)}, u32[]{:S(2)}) collective-permute-start(bf16[4,16,3584]{2,1,0:T(8,128)(2,1)S(1)} %get-tuple-element.18.refs_0_), channel_id=1, source_target_pairs={{0,64},{64,128},{128,192},{192,0},{1,65},{65,129},{129,193},{193,1... | collective-permute-start | bytes 1376264 | tf_op jit(solution)/shard_map/ppermute | solution.py:25
  57.2 15.8 %collective-permute-start.10 = (bf16[4,16,3584]{2,1,0:T(8,128)(2,1)S(1)}, bf16[4,16,3584]{2,1,0:T(8,128)(2,1)}, u32[]{:S(2)}, u32[]{:S(2)}) collective-permute-start(bf16[4,16,3584]{2,1,0:T(8,128)(2,1)S(1)} %get-tuple-element.19.refs_1_), channel_id=1, source_target_pairs={{0,192},{64,0},{128,64},{192,128},{1,193},{65,1},{129,65},{193,129... | collective-permute-start | bytes 1376264 | tf_op jit(solution)/shard_map/ppermute | solution.py:25
  60.9 9.5 %collective-permute-start.29 = (bf16[2,16,3712]{2,1,0:T(8,128)(2,1)}, bf16[2,16,3712]{2,1,0:T(8,128)(2,1)S(1)}, u32[]{:S(2)}, u32[]{:S(2)}) collective-permute-start(bf16[2,16,3712]{2,1,0:T(8,128)(2,1)} %collective-permute-done.25.refs_9_.refs_25_), channel_id=1, source_target_pairs={{0,56},{8,0},{16,8},{24,16},{32,24},{40,32},{48,40},{56,48},{1,57}... | collective-permute-start | bytes 712712 | tf_op jit(solution)/shard_map/ppermute | solution.py:25
  62.9 12.5 %collective-permute-start.30 = (bf16[2,16,3712]{2,1,0:T(8,128)(2,1)}, bf16[2,16,3712]{2,1,0:T(8,128)(2,1)S(1)}, u32[]{:S(2)}, u32[]{:S(2)}) collective-permute-start(bf16[2,16,3712]{2,1,0:T(8,128)(2,1)} %collective-permute-done.26.refs_10_.refs_26_), channel_id=1, source_target_pairs={{0,8},{8,16},{16,24},{24,32},{32,40},{40,48},{48,56},{56,0},{1,9},... | collective-permute-start | bytes 712712 | tf_op jit(solution)/shard_map/ppermute | solution.py:25
  70.3 16.0 %copy-start.11 = (bf16[2,16,3712]{2,1,0:T(8,128)(2,1)}, bf16[2,16,3712]{2,1,0:T(8,128)(2,1)S(1)}, u32[]{:S(2)}) copy-start(bf16[2,16,3712]{2,1,0:T(8,128)(2,1)S(1)} %collective-permute-done.29.refs_13_.refs_29_) | copy-start | bytes 712708
  70.3 35.7 %collective-permute-start.8 = (bf16[4,16,3584]{2,1,0:T(8,128)(2,1)S(1)}, bf16[4,16,3584]{2,1,0:T(8,128)(2,1)}, u32[]{:S(2)}, u32[]{:S(2)}) collective-permute-start(bf16[4,16,3584]{2,1,0:T(8,128)(2,1)S(1)} %get-tuple-element.19.refs_1_), channel_id=1, source_target_pairs={{0,64},{64,128},{128,192},{192,0},{1,65},{65,129},{129,193},{193,1... | collective-permute-start | bytes 1376264 | tf_op jit(solution)/shard_map/ppermute | solution.py:25
  71.5 1.5 %copy-start.14 = (bf16[4,16,3584]{2,1,0:T(8,128)(2,1)}, bf16[4,16,3584]{2,1,0:T(8,128)(2,1)S(1)}, u32[]{:S(2)}) copy-start(bf16[4,16,3584]{2,1,0:T(8,128)(2,1)S(1)} %collective-permute-done.7.refs_2_) | copy-start | bytes 1376260
  71.5 34.5 %collective-permute-start.9 = (bf16[4,16,3584]{2,1,0:T(8,128)(2,1)S(1)}, bf16[4,16,3584]{2,1,0:T(8,128)(2,1)}, u32[]{:S(2)}, u32[]{:S(2)}) collective-permute-start(bf16[4,16,3584]{2,1,0:T(8,128)(2,1)S(1)} %get-tuple-element.18.refs_0_), channel_id=1, source_target_pairs={{0,192},{64,0},{128,64},{192,128},{1,193},{65,1},{129,65},{193,129... | collective-permute-start | bytes 1376264 | tf_op jit(solution)/shard_map/ppermute | solution.py:25
  73.0 13.4 %collective-permute-start.31 = (bf16[2,16,3712]{2,1,0:T(8,128)(2,1)}, bf16[2,16,3712]{2,1,0:T(8,128)(2,1)S(1)}, u32[]{:S(2)}, u32[]{:S(2)}) collective-permute-start(bf16[2,16,3712]{2,1,0:T(8,128)(2,1)} %collective-permute-done.28.refs_12_.refs_28_), channel_id=1, source_target_pairs={{0,56},{8,0},{16,8},{24,16},{32,24},{40,32},{48,40},{56,48},{1,57}... | collective-permute-start | bytes 712712 | tf_op jit(solution)/shard_map/ppermute | solution.py:25
  75.4 10.9 %copy-start.12 = (bf16[2,16,3712]{2,1,0:T(8,128)(2,1)}, bf16[2,16,3712]{2,1,0:T(8,128)(2,1)S(1)}, u32[]{:S(2)}) copy-start(bf16[2,16,3712]{2,1,0:T(8,128)(2,1)S(1)} %collective-permute-done.30.refs_14_.refs_30_) | copy-start | bytes 712708
  75.4 30.6 %collective-permute-start.11 = (bf16[4,16,3584]{2,1,0:T(8,128)(2,1)}, bf16[4,16,3584]{2,1,0:T(8,128)(2,1)}, u32[]{:S(2)}, u32[]{:S(2)}) collective-permute-start(bf16[4,16,3584]{2,1,0:T(8,128)(2,1)} %copy-done.14), channel_id=1, source_target_pairs={{0,64},{64,128},{128,192},{192,0},{1,65},{65,129},{129,193},{193,1... | collective-permute-start | bytes 1376264 | tf_op jit(solution)/shard_map/ppermute | solution.py:25
  75.9 30.1 %collective-permute-start.12 = (bf16[4,16,3584]{2,1,0:T(8,128)(2,1)}, bf16[4,16,3584]{2,1,0:T(8,128)(2,1)}, u32[]{:S(2)}, u32[]{:S(2)}) collective-permute-start(bf16[4,16,3584]{2,1,0:T(8,128)(2,1)} %collective-permute-done.10.refs_5_), channel_id=1, source_target_pairs={{0,192},{64,0},{128,64},{192,128},{1,193},{65,1},{129,65},{193,129... | collective-permute-start | bytes 1376264 | tf_op jit(solution)/shard_map/ppermute | solution.py:25
  86.4 0.7 copy-start.13
  94.8 37.0 %collective-permute-start.32 = (f32[64,3584]{1,0:T(8,128)}, f32[64,3584]{1,0:T(8,128)}, u32[]{:S(2)}, u32[]{:S(2)}) collective-permute-start(f32[64,3584]{1,0:T(8,128)} %get-tuple-element.28.x_ref), channel_id=1, source_target_pairs={{0,4},{4,0},{1,5},{5,1},{2,6},{6,2},{3,7},{7,3},{8,12},{12,8},{9,1... | collective-permute-start | bytes 2752520 | tf_op jit(solution)/shard_map/ppermute | solution.py:25
  113.8 7.5 %copy-start.15 = (f32[4,128,128]{2,1,0:T(8,128)S(1)}, f32[4,128,128]{2,1,0:T(8,128)}, u32[]{:S(2)}) copy-start(f32[4,128,128]{2,1,0:T(8,128)} %get-tuple-element.31) | copy-start | bytes 786436
  113.8 17.9 %copy-start.3 = (f32[64,3584]{1,0:T(8,128)S(1)}, f32[64,3584]{1,0:T(8,128)}, u32[]{:S(2)}) copy-start(f32[64,3584]{1,0:T(8,128)} %get-tuple-element.28.x_ref) | copy-start | bytes 2752516
  113.8 20.0 %collective-permute-start.33 = (f32[64,3584]{1,0:T(8,128)}, f32[64,3584]{1,0:T(8,128)}, u32[]{:S(2)}, u32[]{:S(2)}) collective-permute-start(f32[64,3584]{1,0:T(8,128)} %get-tuple-element.29.x_ref), channel_id=1, source_target_pairs={{0,4},{4,0},{1,5},{5,1},{2,6},{6,2},{3,7},{7,3},{8,12},{12,8},{9,1... | collective-permute-start | bytes 2752520 | tf_op jit(solution)/shard_map/ppermute | solution.py:25
  114.0 17.1 %all-to-all-start.1 = ((f32[8,192,128]{2,1,0:T(8,128)}), f32[8,192,128]{2,1,0:T(8,128)S(1)}, u32[]{:S(2)}, u32[]{:S(2)}) async-start(f32[8,192,128]{2,1,0:T(8,128)} %get-tuple-element.26), calls=%async_computation.1 | async-start | bytes 1572864 | tf_op jit(solution)/shard_map/all_to_all | solution.py:302
  119.8 1.4 %collective-permute-start.34 = (f32[2,128,128]{2,1,0:T(8,128)S(1)}, f32[2,128,128]{2,1,0:T(8,128)S(1)}, u32[]{:S(2)}, u32[]{:S(2)}) collective-permute-start(f32[2,128,128]{2,1,0:T(8,128)S(1)} %slice.19), channel_id=1, source_target_pairs={{0,4},{4,0},{1,5},{5,1},{2,6},{6,2},{3,7},{7,3},{8,12},{12,8},{9,1... | collective-permute-start | bytes 393224 | tf_op jit(solution)/shard_map/ppermute | solution.py:25
  131.7 2.1 %copy-start.4 = (f32[64,3584]{1,0:T(8,128)S(1)}, f32[64,3584]{1,0:T(8,128)}, u32[]{:S(2)}) copy-start(f32[64,3584]{1,0:T(8,128)} %get-tuple-element.29.x_ref) | copy-start | bytes 2752516

commit v2 on v1

v2 whole, which is shorter than its diff:
```python
import functools

import jax
import jax.numpy as jnp
from jax import lax
from jax.experimental import pallas as pl
from jax.experimental.pallas import tpu as pltpu
from jax.sharding import Mesh
from jax.sharding import PartitionSpec as P


DP = ("x", "z", "c")
NX, NZ = 4, 8
bf = jnp.bfloat16
f32 = jnp.float32
CA = 3584
BLK = 1792
GRANT = 18
XS = (0, -1, 1, 2)
ZS = (0, -1, 1, -2, 2, -3, 3, 4)


def shift(a, axis, k):
    n = lax.axis_size(axis)
    return lax.ppermute(a, axis, [(i, (i + k) % n) for i in range(n)])


def tn(a, b):
    return lax.dot_general(a, b, (((0,), (0,)), ((), ())), preferred_element_type=f32)


def kernel_stack(n, per, *refs):
    for k in range(n):
        refs[n + k // per][k % per] = refs[k][...]


def stack(parts, halves):
    vm = pl.BlockSpec(memory_space=pltpu.VMEM)
    n = len(parts)
    per = n // halves
    half = jax.ShapeDtypeStruct((per, *parts[0].shape), parts[0].dtype)
    return pl.pallas_call(
        functools.partial(kernel_stack, n, per),
        in_specs=[vm] * n,
        out_specs=[vm] * halves,
        out_shape=[half] * halves,
        compiler_params=params(8),
        name="stack",
    )(*parts)


def kernel_prep(s_ref, w_ref, wo_ref, at_ref, b_ref, sp_ref, spo_ref, out_ref):
    own = pl.multiple_of(s_ref[2] * 128, 128)
    other = pl.multiple_of(128 - s_ref[2] * 128, 128)
    b2 = jnp.concatenate([b_ref[:, pl.ds(own, 128)], b_ref[:, pl.ds(other, 128)]], axis=1)
    for r in range(0, out_ref.shape[0], BLK):
        rows = slice(r, r + BLK)
        ab = tn(at_ref[:, rows], b2)
        out_ref[rows, :128] = (w_ref[rows, :].astype(f32) + ab[:, :128]).astype(bf)
        out_ref[rows, 128:] = (wo_ref[rows, :].astype(f32) + ab[:, 128:]).astype(bf)
    for j in range(4):

        @pl.when(s_ref[7 + j] > 0)
        def _():
            sp = sp_ref[j] if j < 2 else spo_ref[j - 2]
            at = pl.ds(pl.multiple_of(s_ref[3 + j] * 128, 128), 128)
            cols = slice(0, 128) if j < 2 else slice(128, 256)
            out_ref[at, cols] = (out_ref[at, cols].astype(f32) + sp.astype(f32)).astype(bf)


def assemble(scr, ref_list, places, xi, zi, cols):
    for ref, place in zip(ref_list, places):
        for k, (dx, dz) in enumerate(place):
            row = (lax.rem(xi + dx + NX, NX) * NZ + lax.rem(zi + dz + NZ, NZ)) * 16
            scr[pl.ds(pl.multiple_of(row, 16), 16), :] = ref[k, :, cols]


def picks(base, r, s_ref, scr, cot_ref, gs_ref):
    for j in range(4):
        at = (s_ref[3 + j] - base) * 128 - r

        @pl.when((at >= 0) & (at < BLK))
        def _():
            c = s_ref[2] if j < 2 else 1 - s_ref[2]
            cot = cot_ref[:, pl.ds(pl.multiple_of(c * 128, 128), 128)]
            gs_ref[j] = tn(scr[:, pl.ds(pl.multiple_of(at, 128), 128)], cot)


def kernel_a(places, n, s_ref, *refs):
    chunks = refs[:n]
    w_ref, cot_ref, out_ref, ga_ref, clt_ref, low_ref, gs_ref, scr, ext = refs[n:]
    xi, zi = s_ref[0], s_ref[1]
    assemble(ext, chunks, places, xi, zi, slice(CA, CA + 128))
    low_ref[...] = ext[...]
    clt_ref[...] = ext[...].astype(f32).T.astype(bf)
    gs_ref[...] = jnp.zeros_like(gs_ref)
    for t, r in enumerate(range(0, CA, BLK)):
        buf = scr.at[t % 2]
        assemble(buf, chunks, places, xi, zi, slice(r, r + BLK))
        h = buf[...]
        part = jnp.dot(h, w_ref[r : r + BLK, :], preferred_element_type=f32)
        out_ref[...] = part if t == 0 else out_ref[...] + part
        ga_ref[:, r : r + BLK] = jnp.dot(clt_ref[:64, :], h, preferred_element_type=f32)
        picks(0, r, s_ref, buf, cot_ref, gs_ref)


def kernel_b(places, n, cb, s_ref, *refs):
    chunks = refs[:n]
    w_ref, cot_ref, outa_ref, clt_ref, low_ref, gsa_ref, send_ref, ga_ref, gs_ref, scr, acc = refs[n:]
    xi, zi, ci = s_ref[0], s_ref[1], s_ref[2]
    gs_ref[...] = gsa_ref[...]
    for t, r in enumerate(range(0, cb, BLK)):
        buf = scr.at[t % 2]
        assemble(buf, chunks, places, xi, zi, slice(r, r + BLK))
        h = buf[...]
        part = jnp.dot(h, w_ref[CA + r : CA + r + BLK, :], preferred_element_type=f32)
        acc[...] = (outa_ref[...] if t == 0 else acc[...]) + part
        ga_ref[:, r : r + BLK] = jnp.dot(clt_ref[:64, :], h, preferred_element_type=f32)
        picks(CA // 128, r, s_ref, buf, cot_ref, gs_ref)
    gb = tn(low_ref[...], cot_ref[...])[64:]
    for j in range(2):
        c = ci if j == 0 else 1 - ci
        for y in range(4):
            send_ref[c * 4 + y, :128, :] = acc[y * 128 : (y + 1) * 128, j * 128 : (j + 1) * 128].astype(bf)
            send_ref[j * 4 + y, 128:, :] = gb[:, j * 128 : (j + 1) * 128].astype(bf)


def kernel_final(got_ref, mixed_ref, gb_ref):
    acc = None
    for c in range(2):
        s = got_ref[c * 4].astype(f32)
        for y in range(1, 4):
            s = s + got_ref[c * 4 + y].astype(f32)
        for z in range(NZ):
            mixed_ref[z, c] = s[z * 16 : (z + 1) * 16].astype(bf)
        acc = s[128:] if acc is None else acc + s[128:]
    gb_ref[...] = acc


def kernel_add(x_ref, y_ref, o_ref):
    o_ref[...] = x_ref[...] + y_ref[...]


def kernel_add_to(_, x_ref, y_ref, o_ref):
    o_ref[...] = x_ref[...] + y_ref[...]


def params(mib=24):
    return pltpu.CompilerParams(vmem_limit_bytes=mib << 20)


def shards(gate, up, cot, w, a, b, sbv, rows, cols, counts):
    xi, zi, ci = lax.axis_index("x"), lax.axis_index("z"), lax.axis_index("c")
    chip = xi * NZ + zi
    K = w.shape[0]
    CB = K - CA
    first = ci == 0
    hid = (jax.nn.silu(gate.astype(f32)) * up.astype(f32)).astype(bf)
    own_b = hid[:, CA:]
    cl = lax.dot_general(cot, b, (((1,), (1,)), ((), ())), preferred_element_type=f32).astype(bf)
    lo = jnp.dot(hid, a, preferred_element_type=f32).astype(bf)
    own_a = jnp.concatenate([hid[:, :CA], cl, lo], axis=1)
    fb, bb = [own_b], [own_b]
    for _ in range(1, 4):
        fb.append(shift(fb[-1], "z", 1))
        bb.append(shift(bb[-1], "z", -1))
    sb = stack([own_b, fb[1], bb[1], fb[2], bb[2], fb[3], bb[3], shift(bb[3], "z", -1)], 2)
    sa = stack([own_a, shift(own_a, "x", 1), shift(own_a, "x", -1), shift(own_a, "x", 2)], 2)
    chunks_a, places_a = list(sa), [[(x, 0) for x in XS[:2]], [(x, 0) for x in XS[2:]]]
    f, r = list(sa), list(sa)
    for k in range(1, 5):
        for h in (0, 1):
            if k < 4 or h == 0:
                f[h] = shift(f[h], "z", 1)
                chunks_a.append(f[h])
                places_a.append([(x, -k) for x in XS[2 * h : 2 * h + 2]])
        for h in (1, 0):
            if k < 4 or h == 1:
                r[h] = shift(r[h], "z", -1)
                chunks_a.append(r[h])
                places_a.append([(x, k) for x in XS[2 * h : 2 * h + 2]])
    xf = [shift(sb[0], "x", 1), shift(sb[1], "x", 1)]
    xb = [shift(sb[0], "x", -1), shift(sb[1], "x", -1)]
    chunks_b = [*sb, *xf, *xb, shift(xf[0], "x", 1), shift(xb[1], "x", -1)]
    zs = [list(ZS[:4]), list(ZS[4:])]
    places_b = [[(x, z) for z in zs[h]] for x in XS for h in (0, 1)]
    sp = sbv[0, 0]
    w_o = shift(w, "c", 1)
    sp_o = shift(sp, "c", 1)
    b2 = lax.dynamic_slice_in_dim(b, chip * 256, 256, 1)
    r2 = lax.dynamic_slice_in_dim(rows[:, 0, :], chip * 2, 2, 0)
    live = jnp.arange(2, dtype=jnp.int32)[None, :] < lax.dynamic_slice_in_dim(counts[:, 0], chip * 2, 2, 0)[:, None]
    rel = jnp.where(first, r2, r2[::-1])
    rlive = jnp.where(first, live, live[::-1])
    scal = jnp.concatenate(
        [jnp.stack([xi, zi, ci]).astype(jnp.int32), rel.reshape(4), rlive.astype(jnp.int32).reshape(4)]
    )
    cc = lax.all_to_all(cot.reshape(16, 32, 256), ("x", "z"), split_axis=1, concat_axis=0)
    cc = cc.reshape(512, 256)

    vm = pl.BlockSpec(memory_space=pltpu.VMEM)
    sm = pl.BlockSpec(memory_space=pltpu.SMEM)
    cost = pl.CostEstimate(flops=2 * 512 * CA * 320, bytes_accessed=8 << 20, transcendentals=0)
    weff = pl.pallas_call(
        kernel_prep,
        in_specs=[sm] + [vm] * 6,
        out_specs=vm,
        out_shape=jax.ShapeDtypeStruct((K, 256), bf),
        compiler_params=params(GRANT),
        cost_estimate=pl.CostEstimate(flops=1 << 28, bytes_accessed=8 << 20, transcendentals=0),
        name="prep",
    )(scal, w, w_o, a.T, b2, sp, sp_o)
    na, nb = len(chunks_a), len(chunks_b)
    out_a, ga_a, clt, low, gs_a = pl.pallas_call(
        functools.partial(kernel_a, places_a, na),
        in_specs=[sm] + [vm] * (na + 2),
        out_specs=[vm] * 5,
        out_shape=[
            jax.ShapeDtypeStruct((512, 256), f32),
            jax.ShapeDtypeStruct((64, CA), f32),
            jax.ShapeDtypeStruct((128, 512), bf),
            jax.ShapeDtypeStruct((512, 128), bf),
            jax.ShapeDtypeStruct((4, 128, 128), f32),
        ],
        scratch_shapes=[pltpu.VMEM((2, 512, BLK), bf), pltpu.VMEM((512, 128), bf)],
        compiler_params=params(GRANT),
        cost_estimate=cost,
        name="colour_a",
    )(scal, *chunks_a, weff, cc)
    send, ga_b, gs = pl.pallas_call(
        functools.partial(kernel_b, places_b, nb, CB),
        in_specs=[sm] + [vm] * (nb + 6),
        out_specs=[vm] * 3,
        out_shape=[
            jax.ShapeDtypeStruct((8, 192, 128), bf),
            jax.ShapeDtypeStruct((64, CB), f32),
            jax.ShapeDtypeStruct((4, 128, 128), f32),
        ],
        scratch_shapes=[pltpu.VMEM((2, 512, BLK), bf), pltpu.VMEM((512, 256), f32)],
        compiler_params=params(GRANT),
        cost_estimate=cost,
        name="colour_b",
    )(scal, *chunks_b, weff, cc, out_a, clt, low, gs_a)
    got = lax.all_to_all(send, ("c", "y"), 0, 0, tiled=True)
    gsum = gs[:2] + shift(gs[2:], "c", 1)
    grad_blocks = jnp.where(rlive[0][:, None, None], gsum, 0.0)[None, None]
    left = pl.BlockSpec((64, CA // 2), lambda i: (0, i))
    ga_ao = shift(ga_a, "c", 1)
    ga_bo = shift(ga_b, "c", 1)
    grad_a = pl.pallas_call(
        kernel_add,
        grid=(2,),
        in_specs=[left, left],
        out_specs=left,
        out_shape=jax.ShapeDtypeStruct((64, K), f32),
        compiler_params=params(8),
        name="add_a",
    )(ga_a, ga_ao)
    grad_a = pl.pallas_call(
        kernel_add_to,
        grid=(2,),
        in_specs=[pl.BlockSpec(memory_space=pl.ANY), left, left],
        out_specs=pl.BlockSpec((64, CA // 2), lambda i: (0, i + 2)),
        out_shape=jax.ShapeDtypeStruct((64, K), f32),
        input_output_aliases={0: 0},
        compiler_params=params(8),
        name="add_b",
    )(grad_a, ga_b, ga_bo).T
    mixed, grad_b = pl.pallas_call(
        kernel_final,
        in_specs=[vm],
        out_specs=[vm, vm],
        out_shape=[jax.ShapeDtypeStruct((NZ, 2, 16, 128), bf), jax.ShapeDtypeStruct((64, 128), f32)],
        compiler_params=params(),
        name="final",
    )(got)
    return (mixed.reshape(256, 128), grad_a, grad_b, grad_blocks)


def solution(mesh):
    finer = Mesh(mesh.devices.reshape(4, 8, 2, 4), ("x", "z", "c", "y"))
    in_specs = (
        P(DP, "y"),
        P(DP, "y"),
        P(DP, None),
        P("y", DP),
        P("y", None),
        P(),
        P(DP, "y", None, None, None),
        P(None, "y", None),
        P(None, "y", None),
        P(None, "y"),
    )
    out_specs = (P("y", DP), P("y", None), P(None, DP), P(DP, "y", None, None, None))
    return jax.shard_map(shards, mesh=finer, in_specs=in_specs, out_specs=out_specs, check_vma=False)
```

time: 136 us -> 133 us (0.978)
  local copies, waits for them, and re-layouts: 4.4 us -> 24.2 us
  waiting for transfers between devices: 31.6 us -> 21 us
  Pallas kernels: 27.1 us -> 18.9 us
  starting transfers between devices: 68.1 us -> 63.8 us
    unnamed x41 -> x69, local copies, waits for them, and re-layouts: 0.82 us -> 22.7 us
    ppermute x35, waiting for transfers between devices: 22.5 us -> 13.8 us  [shift(): return lax.ppermute(a, axis, [(i, (i + k) % n) for i in range(n)])]
    pallas_call x7, Pallas kernels: 26.4 us -> 18.2 us  [the longest x1 5.93 us: shards(): pl.pallas_call(functools.partial(kernel_b, places_b, nb, CB), in_specs=[s...]
    all_to_all x1, starting transfers between devices: 9.5 us -> 5.91 us  [shards(): lax.all_to_all(cot.reshape(16, 32, 256), ('x', 'z'), split_axis=1, concat...]
    all_to_all x1, waiting for transfers between devices: 9.06 us -> 7.19 us  [shards(): got = lax.all_to_all(send, ('c', 'y'), 0, 0, tiled=True)]
  transfers between devices with their start and end apart: 37 -> 37, of which waited for: 11 -> 10; matrix products, arithmetic and copies ran while one was open for 5% -> 5% of each run, Pallas kernels for 18% -> 13%
where the time goes in v2:
time: 133 us
  starting transfers between devices  63.8 us (48%)
  local copies, waits for them, and re-layouts  24.2 us (18%)
  waiting for transfers between devices  21 us (16%)
  Pallas kernels  18.9 us (14%)
  other arithmetic  2.07 us (2%)
  matrix products  1.66 us (1%)
    ppermute x35, starting transfers between devices, shift(): return lax.ppermute(a, axis, [(i, (i + k) % n) for i in range(n)])  53.3 us
    unnamed x69, local copies, waits for them, and re-layouts  22.7 us
    ppermute x35, waiting for transfers between devices, shift(): return lax.ppermute(a, axis, [(i, (i + k) % n) for i in range(n)])  13.8 us
    all_to_all x1, waiting for transfers between devices, shards(): got = lax.all_to_all(send, ('c', 'y'), 0, 0, tiled=True)  7.19 us
    pallas_call x1, Pallas kernels, shards(): pl.pallas_call(functools.partial(kernel_b, places_b, nb, CB), in_specs=[s...  5.93 us
    all_to_all x1, starting transfers between devices, shards(): lax.all_to_all(cot.reshape(16, 32, 256), ('x', 'z'), split_axis=1, concat...  5.91 us
    all_to_all x1, starting transfers between devices, shards(): got = lax.all_to_all(send, ('c', 'y'), 0, 0, tiled=True)  4.6 us
    pallas_call x1, Pallas kernels, shards(): pl.pallas_call(functools.partial(kernel_a, places_a, na), in_specs=[sm] +...  4.3 us
  transfers between devices with their start and end apart: 37, of which 10 were waited for; matrix products, arithmetic and copies ran while one was open for 5% of the time, Pallas kernels for 13%

profile of v2, /device:TPU:1, one launch (start us, length us, event | category | flops | bytes accessed | tf_op | source)
XLA Modules:
  0.0 132.6 jit_solution(17124099452567329946)
XLA Ops:
  0.7 3.3 %collective-permute-start.13 = (bf16[7168,128]{1,0:T(8,128)(2,1)}, bf16[7168,128]{1,0:T(8,128)(2,1)}, u32[]{:S(2)}, u32[]{:S(2)}) collective-permute-start(bf16[7168,128]{1,0:T(8,128)(2,1)} %w_ref.1), channel_id=1, source_target_pairs={{0,4},{4,0},{1,5},{5,1},{2,6},{6,2},{3,7},{7,3},{8,12},{12,8},{9,1... | collective-permute-start | bytes 5505032 | tf_op jit(solution)/shard_map/ppermute | solution.py:25
  3.9 1.2 fusion.4
  5.2 3.9 %collective-permute-start.1 = (bf16[16,3584]{1,0:T(8,128)(2,1)S(1)}, bf16[16,3584]{1,0:T(8,128)(2,1)S(1)}, u32[]{:S(2)}, u32[]{:S(2)}) collective-permute-start(bf16[16,3584]{1,0:T(8,128)(2,1)S(1)} %get-tuple-element.35.refs_0_), channel_id=1, source_target_pairs={{0,56},{8,0},{16,8},{24,16},{32,24},{40,32},{48,40},{56,48},{1,57}... | collective-permute-start | bytes 344072 | tf_op jit(solution)/shard_map/ppermute | solution.py:25
  9.1 1.3 convolution_convert_fusion.1
  10.9 1.2 collective-permute-start.15
  12.1 1.5 %collective-permute-start.16 = (bf16[16,3712]{1,0:T(8,128)(2,1)S(1)}, bf16[16,3712]{1,0:T(8,128)(2,1)S(1)}, u32[]{:S(2)}, u32[]{:S(2)}) collective-permute-start(bf16[16,3712]{1,0:T(8,128)(2,1)S(1)} %concatenate.7.refs_0_), channel_id=1, source_target_pairs={{0,192},{64,0},{128,64},{192,128},{1,193},{65,1},{129,65},{193,129... | collective-permute-start | bytes 356360 | tf_op jit(solution)/shard_map/ppermute | solution.py:25
  13.6 1.5 %collective-permute-start.17 = (bf16[16,3712]{1,0:T(8,128)(2,1)S(1)}, bf16[16,3712]{1,0:T(8,128)(2,1)S(1)}, u32[]{:S(2)}, u32[]{:S(2)}) collective-permute-start(bf16[16,3712]{1,0:T(8,128)(2,1)S(1)} %concatenate.7.refs_0_), channel_id=1, source_target_pairs={{0,128},{64,192},{128,0},{192,64},{1,129},{65,193},{129,1},{193,65... | collective-permute-start | bytes 356360 | tf_op jit(solution)/shard_map/ppermute | solution.py:25
  15.1 2.2 %collective-permute-done.refs_1_ = bf16[16,3584]{1,0:T(8,128)(2,1)S(1)} collective-permute-done((bf16[16,3584]{1,0:T(8,128)(2,1)S(1)}, bf16[16,3584]{1,0:T(8,128)(2,1)S(1)}, u32[]{:S(2)}, u32[]{:S(2)}) %collective-permute-start) | collective-permute-done | bytes 114720 | tf_op jit(solution)/shard_map/ppermute | solution.py:25
  17.8 1.0 collective-permute-start.2
  18.8 1.2 collective-permute-done.17.refs_3_
  20.2 0.8 collective-permute-done.3.refs_4_
  21.0 2.0 %collective-permute-start.5 = (bf16[16,3584]{1,0:T(8,128)(2,1)S(1)}, bf16[16,3584]{1,0:T(8,128)(2,1)S(1)}, u32[]{:S(2)}, u32[]{:S(2)}) collective-permute-start(bf16[16,3584]{1,0:T(8,128)(2,1)S(1)} %collective-permute-done.3.refs_4_), channel_id=1, source_target_pairs={{0,56},{8,0},{16,8},{24,16},{32,24},{40,32},{48,40},{56,48},{1,57}... | collective-permute-start | bytes 344072 | tf_op jit(solution)/shard_map/ppermute | solution.py:25
  23.0 0.6 copy-done.18
  23.6 0.6 copy-done.20
  24.3 3.3 %collective-permute-start.14 = (bf16[2,128,128]{2,1,0:T(8,128)(2,1)S(1)}, bf16[2,128,128]{2,1,0:T(8,128)(2,1)S(1)}, u32[]{:S(2)}, u32[]{:S(2)}) collective-permute-start(bf16[2,128,128]{2,1,0:T(8,128)(2,1)S(1)} %bitcast.30), channel_id=1, source_target_pairs={{0,4},{4,0},{1,5},{5,1},{2,6},{6,2},{3,7},{7,3},{8,12},{12,8},{9,1... | collective-permute-start | bytes 196616 | tf_op jit(solution)/shard_map/ppermute | solution.py:25
  27.6 0.9 collective-permute-done.14.spo_ref
  29.1 2.8 %collective-permute-start.20 = (bf16[2,16,3712]{2,1,0:T(8,128)(2,1)S(1)}, bf16[2,16,3712]{2,1,0:T(8,128)(2,1)S(1)}, u32[]{:S(2)}, u32[]{:S(2)}) collective-permute-start(bf16[2,16,3712]{2,1,0:T(8,128)(2,1)S(1)} %get-tuple-element.21.refs_1_), channel_id=1, source_target_pairs={{0,56},{8,0},{16,8},{24,16},{32,24},{40,32},{48,40},{56,48},{1,57}... | collective-permute-start | bytes 712712 | tf_op jit(solution)/shard_map/ppermute | solution.py:25
  32.6 2.7 %collective-permute-start.21 = (bf16[2,16,3712]{2,1,0:T(8,128)(2,1)S(1)}, bf16[2,16,3712]{2,1,0:T(8,128)(2,1)}, u32[]{:S(2)}, u32[]{:S(2)}) collective-permute-start(bf16[2,16,3712]{2,1,0:T(8,128)(2,1)S(1)} %get-tuple-element.20.refs_0_), channel_id=1, source_target_pairs={{0,56},{8,0},{16,8},{24,16},{32,24},{40,32},{48,40},{56,48},{1,57}... | collective-permute-start | bytes 712712 | tf_op jit(solution)/shard_map/ppermute | solution.py:25
  35.3 1.4 %collective-permute-done.20.refs_4_ = bf16[2,16,3712]{2,1,0:T(8,128)(2,1)S(1)} collective-permute-done((bf16[2,16,3712]{2,1,0:T(8,128)(2,1)S(1)}, bf16[2,16,3712]{2,1,0:T(8,128)(2,1)S(1)}, u32[]{:S(2)}, u32[]{:S(2)}) %collective-permute-start.20) | collective-permute-done | bytes 237600 | tf_op jit(solution)/shard_map/ppermute | solution.py:25
  36.7 3.4 %collective-permute-start.6 = (bf16[16,3584]{1,0:T(8,128)(2,1)S(1)}, bf16[16,3584]{1,0:T(8,128)(2,1)S(1)}, u32[]{:S(2)}, u32[]{:S(2)}) collective-permute-start(bf16[16,3584]{1,0:T(8,128)(2,1)S(1)} %collective-permute-done.5.refs_6_), channel_id=1, source_target_pairs={{0,56},{8,0},{16,8},{24,16},{32,24},{40,32},{48,40},{56,48},{1,57}... | collective-permute-start | bytes 344072 | tf_op jit(solution)/shard_map/ppermute | solution.py:25
  40.8 1.0 collective-permute-done.21.refs_5_
  42.3 2.0 %collective-permute-done.6.refs_7_ = bf16[16,3584]{1,0:T(8,128)(2,1)S(1)} collective-permute-done((bf16[16,3584]{1,0:T(8,128)(2,1)S(1)}, bf16[16,3584]{1,0:T(8,128)(2,1)S(1)}, u32[]{:S(2)}, u32[]{:S(2)}) %collective-permute-start.6) | collective-permute-done | bytes 114720 | tf_op jit(solution)/shard_map/ppermute | solution.py:25
  44.3 0.6 copy-done.26
  44.9 3.4 %collective-permute-start.25 = (bf16[2,16,3712]{2,1,0:T(8,128)(2,1)}, bf16[2,16,3712]{2,1,0:T(8,128)(2,1)}, u32[]{:S(2)}, u32[]{:S(2)}) collective-permute-start(bf16[2,16,3712]{2,1,0:T(8,128)(2,1)} %collective-permute-done.21.refs_5_), channel_id=1, source_target_pairs={{0,56},{8,0},{16,8},{24,16},{32,24},{40,32},{48,40},{56,48},{1,57}... | collective-permute-start | bytes 712712 | tf_op jit(solution)/shard_map/ppermute | solution.py:25
  48.4 1.0 copy.19
  49.4 0.9 copy.18
  50.2 5.9 %all-to-all-start = ((bf16[1,16,32,256]{3,1,0,2:T(8,128)(2,1)}), bf16[1,16,32,256]{3,1,0,2:T(8,128)(2,1)S(1)}, u32[]{:S(2)}, u32[]{:S(2)}) async-start(bf16[1,16,32,256]{3,1,0,2:T(8,128)(2,1)} %copy.18), calls=%async_computation | async-start | bytes 524288 | tf_op jit(solution)/shard_map/all_to_all | solution.py:198
  56.2 2.5 %collective-permute-start.28 = (bf16[2,16,3712]{2,1,0:T(8,128)(2,1)}, bf16[2,16,3712]{2,1,0:T(8,128)(2,1)}, u32[]{:S(2)}, u32[]{:S(2)}) collective-permute-start(bf16[2,16,3712]{2,1,0:T(8,128)(2,1)} %collective-permute-done.24.refs_8_), channel_id=1, source_target_pairs={{0,56},{8,0},{16,8},{24,16},{32,24},{40,32},{48,40},{56,48},{1,57}... | collective-permute-start | bytes 712712 | tf_op jit(solution)/shard_map/ppermute | solution.py:25
  58.8 0.9 copy-done.17
  59.7 0.9 copy-done.19
  60.6 0.9 copy-done.21
  61.5 0.9 copy-done.23
  62.4 0.9 copy-done.25
  63.3 0.9 copy-done.27
  64.2 1.0 stack.14
  65.2 1.2 collective-permute-start.7
  66.4 1.5 %collective-permute-start.10 = (bf16[4,16,3584]{2,1,0:T(8,128)(2,1)}, bf16[4,16,3584]{2,1,0:T(8,128)(2,1)}, u32[]{:S(2)}, u32[]{:S(2)}) collective-permute-start(bf16[4,16,3584]{2,1,0:T(8,128)(2,1)} %get-tuple-element.19.refs_1_), channel_id=1, source_target_pairs={{0,192},{64,0},{128,64},{192,128},{1,193},{65,1},{129,65},{193,129... | collective-permute-start | bytes 1376264 | tf_op jit(solution)/shard_map/ppermute | solution.py:25
  67.9 2.7 %collective-permute-start.29 = (bf16[2,16,3712]{2,1,0:T(8,128)(2,1)}, bf16[2,16,3712]{2,1,0:T(8,128)(2,1)}, u32[]{:S(2)}, u32[]{:S(2)}) collective-permute-start(bf16[2,16,3712]{2,1,0:T(8,128)(2,1)} %collective-permute-done.25.refs_9_), channel_id=1, source_target_pairs={{0,56},{8,0},{16,8},{24,16},{32,24},{40,32},{48,40},{56,48},{1,57}... | collective-permute-start | bytes 712712 | tf_op jit(solution)/shard_map/ppermute | solution.py:25
  70.6 0.7 copy-done.14
  71.5 2.4 %collective-permute-done.29.refs_13_ = bf16[2,16,3712]{2,1,0:T(8,128)(2,1)} collective-permute-done((bf16[2,16,3712]{2,1,0:T(8,128)(2,1)}, bf16[2,16,3712]{2,1,0:T(8,128)(2,1)}, u32[]{:S(2)}, u32[]{:S(2)}) %collective-permute-start.29) | collective-permute-done | bytes 237600 | tf_op jit(solution)/shard_map/ppermute | solution.py:25
  74.0 0.7 collective-permute-start.8
  74.7 1.7 %collective-permute-done.7.refs_2_ = bf16[4,16,3584]{2,1,0:T(8,128)(2,1)} collective-permute-done((bf16[4,16,3584]{2,1,0:T(8,128)(2,1)}, bf16[4,16,3584]{2,1,0:T(8,128)(2,1)}, u32[]{:S(2)}, u32[]{:S(2)}) %collective-permute-start.7) | collective-permute-done | bytes 458784 | tf_op jit(solution)/shard_map/ppermute | solution.py:25
  77.0 3.1 %collective-permute-start.31 = (bf16[2,16,3712]{2,1,0:T(8,128)(2,1)}, bf16[2,16,3712]{2,1,0:T(8,128)(2,1)}, u32[]{:S(2)}, u32[]{:S(2)}) collective-permute-start(bf16[2,16,3712]{2,1,0:T(8,128)(2,1)} %collective-permute-done.28.refs_12_), channel_id=1, source_target_pairs={{0,56},{8,0},{16,8},{24,16},{32,24},{40,32},{48,40},{56,48},{1,57}... | collective-permute-start | bytes 712712 | tf_op jit(solution)/shard_map/ppermute | solution.py:25
  80.1 2.7 %collective-permute-start.12 = (bf16[4,16,3584]{2,1,0:T(8,128)(2,1)}, bf16[4,16,3584]{2,1,0:T(8,128)(2,1)}, u32[]{:S(2)}, u32[]{:S(2)}) collective-permute-start(bf16[4,16,3584]{2,1,0:T(8,128)(2,1)} %collective-permute-done.10.refs_5_), channel_id=1, source_target_pairs={{0,192},{64,0},{128,64},{192,128},{1,193},{65,1},{129,65},{193,129... | collective-permute-start | bytes 1376264 | tf_op jit(solution)/shard_map/ppermute | solution.py:25
  83.1 1.5 %copy-done.5 = bf16[7168,128]{1,0:T(8,128)(2,1)S(1)} copy-done((bf16[7168,128]{1,0:T(8,128)(2,1)S(1)}, bf16[7168,128]{1,0:T(8,128)(2,1)}, u32[]{:S(2)}) %copy-start.5) | copy-done | bytes 1835032
  84.6 0.8 copy-done.29
  85.4 0.8 copy-done.31
  86.3 2.7 %prep.1.refs_16_.refs_8_ = bf16[7168,256]{1,0:T(8,128)(2,1)S(1)} custom-call(s32[11]{0:T(128)S(1)} %concatenate.6.s_ref, bf16[7168,128]{1,0:T(8,128)(2,1)S(1)} %copy-done.5, bf16[7168,128]{1,0:T(8,128)(2,1)} %collective-permute-done.13.wo_ref, bf16[64,7168]{1,0:T(8,128)(2,1)S(1)} %bitcast.27, bf16[64,256]{1,0:T(8,128)(2,1)S(1)} %constant_dynamic-slice_fusion.b_ref, ...), custom_call_target="tpu_custom_call" | custom-call | flops 268435456 | bytes 8388608 | tf_op jit(solution)/shard_map/prep/pallas_call | solution.py:204
  89.0 1.8 %copy-done.1 = bf16[7168,256]{1,0:T(8,128)(2,1)} copy-done((bf16[7168,256]{1,0:T(8,128)(2,1)}, bf16[7168,256]{1,0:T(8,128)(2,1)S(1)}, u32[]{:S(2)}) %copy-start.1) | copy-done | bytes 3670040
  90.8 2.0 %copy-done.2 = bf16[7168,256]{1,0:T(8,128)(2,1)S(1)} copy-done((bf16[7168,256]{1,0:T(8,128)(2,1)S(1)}, bf16[7168,256]{1,0:T(8,128)(2,1)}, u32[]{:S(2)}) %copy-start.2) | copy-done | bytes 3670040
  92.9 0.9 copy-done.7
  93.8 0.9 copy-done.9
  94.8 0.9 copy-done.11
  95.7 0.9 copy-done.13
  96.6 0.9 copy-done.15
  97.6 4.3 %colour_a.1 = (f32[512,256]{1,0:T(8,128)S(1)}, f32[64,3584]{1,0:T(8,128)S(1)}, bf16[128,512]{1,0:T(8,128)(2,1)S(1)}, bf16[512,128]{1,0:T(8,128)(2,1)S(1)}, f32[4,128,128]{2,1,0:T(8,128)S(1)}) custom-call(s32[11]{0:T(128)S(1)} %concatenate.6.s_ref, bf16[2,16,3712]{2,1,0:T(8,128)(2,1)S(1)} %get-tuple-element.20.refs_0_, bf16[2,16,3712]{2,1,0:T(8,128)(2,1)S(1)} %copy-done.7, ...), custom_call_target="tpu_custom_call" | custom-call | flops 1174405120 | bytes 8388608 | tf_op jit(solution)/shard_map/colour_a/pallas_call | solution.py:214
  101.9 6.6 %collective-permute-start.32 = (f32[64,3584]{1,0:T(8,128)S(1)}, f32[64,3584]{1,0:T(8,128)}, u32[]{:S(2)}, u32[]{:S(2)}) collective-permute-start(f32[64,3584]{1,0:T(8,128)S(1)} %get-tuple-element.28.x_ref), channel_id=1, source_target_pairs={{0,4},{4,0},{1,5},{5,1},{2,6},{6,2},{3,7},{7,3},{8,12},{12,8},{9,1... | collective-permute-start | bytes 2752520 | tf_op jit(solution)/shard_map/ppermute | solution.py:25
  108.5 5.9 %colour_b.1 = (bf16[8,192,128]{2,1,0:T(8,128)(2,1)}, f32[64,3584]{1,0:T(8,128)}, f32[4,128,128]{2,1,0:T(8,128)S(1)}) custom-call(s32[11]{0:T(128)S(1)} %concatenate.6.s_ref, bf16[4,16,3584]{2,1,0:T(8,128)(2,1)} %get-tuple-element.18.refs_0_, bf16[4,16,3584]{2,1,0:T(8,128)(2,1)} %get-tuple-element.19.refs_1_, ...), custom_call_target="tpu_custom_call" | custom-call | flops 1174405120 | bytes 8388608 | tf_op jit(solution)/shard_map/colour_b/pallas_call | solution.py:230
  115.1 4.6 %all-to-all-start.1 = ((bf16[8,192,128]{2,1,0:T(8,128)(2,1)}), bf16[8,192,128]{2,1,0:T(8,128)(2,1)S(1)}, u32[]{:S(2)}, u32[]{:S(2)}) async-start(bf16[8,192,128]{2,1,0:T(8,128)(2,1)} %get-tuple-element.26), calls=%async_computation.1 | async-start | bytes 786432 | tf_op jit(solution)/shard_map/all_to_all | solution.py:244
  119.7 0.7 select_bitcast_fusion
  120.4 7.2 %all-to-all-done.1.got_ref = bf16[8,192,128]{2,1,0:T(8,128)(2,1)S(1)} async-done(((bf16[8,192,128]{2,1,0:T(8,128)(2,1)}), bf16[8,192,128]{2,1,0:T(8,128)(2,1)S(1)}, u32[]{:S(2)}, u32[]{:S(2)}) %all-to-all-start.1) | async-done | bytes 393248 | tf_op jit(solution)/shard_map/all_to_all | solution.py:244
  127.6 0.7 final.1
  128.3 2.0 %add_a.1._ = f32[64,7168]{1,0:T(8,128)} custom-call(f32[64,3584]{1,0:T(8,128)S(1)} %get-tuple-element.28.x_ref, f32[64,3584]{1,0:T(8,128)} %collective-permute-done.32.y_ref), custom_call_target="tpu_custom_call" | custom-call | tf_op jit(solution)/shard_map/add_a/pallas_call | solution.py:250
  130.3 2.3 %add_b.1 = f32[64,7168]{1,0:T(8,128)} custom-call(f32[64,7168]{1,0:T(8,128)} %add_a.1._, f32[64,3584]{1,0:T(8,128)} %get-tuple-element.29.x_ref, f32[64,3584]{1,0:T(8,128)} %collective-permute-done.33.y_ref), custom_call_target="tpu_custom_call", output_to_operand_aliasing={{}: (0, {})} | custom-call | tf_op jit(solution)/shard_map/add_b/pallas_call | solution.py:259
  (108 shorter events, 5.5 us)
Async XLA Ops:
  0.6 8.5 %copy-start = (bf16[64,8192]{1,0:T(8,128)(2,1)S(1)}, bf16[64,8192]{1,0:T(8,128)(2,1)}, u32[]{:S(2)}) copy-start(bf16[64,8192]{1,0:T(8,128)(2,1)} %param.15) | copy-start | bytes 3145732
  0.6 9.8 %copy-start.4 = (bf16[7168,64]{0,1:T(8,128)(2,1)S(1)}, bf16[7168,64]{0,1:T(8,128)(2,1)}, u32[]{:S(2)}) copy-start(bf16[7168,64]{0,1:T(8,128)(2,1)} %param.14) | copy-start | bytes 2752516
  0.7 79.4 %collective-permute-start.13 = (bf16[7168,128]{1,0:T(8,128)(2,1)}, bf16[7168,128]{1,0:T(8,128)(2,1)}, u32[]{:S(2)}, u32[]{:S(2)}) collective-permute-start(bf16[7168,128]{1,0:T(8,128)(2,1)} %w_ref.1), channel_id=1, source_target_pairs={{0,4},{4,0},{1,5},{5,1},{2,6},{6,2},{3,7},{7,3},{8,12},{12,8},{9,1... | collective-permute-start | bytes 5505032 | tf_op jit(solution)/shard_map/ppermute | solution.py:25
  5.1 19.1 %copy-start.28 = (bf16[1,1,2,128,128]{4,3,2,1,0:T(8,128)(2,1)S(1)}, bf16[1,1,2,128,128]{4,3,2,1,0:T(8,128)(2,1)}, u32[]{:S(2)}) copy-start(bf16[1,1,2,128,128]{4,3,2,1,0:T(8,128)(2,1)} %param.16) | copy-start | bytes 196612
  5.2 8.4 %collective-permute-start.1 = (bf16[16,3584]{1,0:T(8,128)(2,1)S(1)}, bf16[16,3584]{1,0:T(8,128)(2,1)S(1)}, u32[]{:S(2)}, u32[]{:S(2)}) collective-permute-start(bf16[16,3584]{1,0:T(8,128)(2,1)S(1)} %get-tuple-element.35.refs_0_), channel_id=1, source_target_pairs={{0,56},{8,0},{16,8},{24,16},{32,24},{40,32},{48,40},{56,48},{1,57}... | collective-permute-start | bytes 344072 | tf_op jit(solution)/shard_map/ppermute | solution.py:25
  10.4 48.3 %copy-start.33 = (s32[64,1]{0,1:T(1,128)S(1)}, s32[64,1]{0,1:T(1,128)}, u32[]{:S(2)}) copy-start(s32[64,1]{0,1:T(1,128)} %param.18) | copy-start | bytes 772
  10.8 60.5 %copy-start.32 = (s32[64,1,2]{0,2,1:T(2,128)S(1)}, s32[64,1,2]{0,2,1:T(2,128)}, u32[]{:S(2)}) copy-start(s32[64,1,2]{0,2,1:T(2,128)} %param.17) | copy-start | bytes 1540
  10.9 6.9 %collective-permute-start.15 = (bf16[16,3712]{1,0:T(8,128)(2,1)S(1)}, bf16[16,3712]{1,0:T(8,128)(2,1)S(1)}, u32[]{:S(2)}, u32[]{:S(2)}) collective-permute-start(bf16[16,3712]{1,0:T(8,128)(2,1)S(1)} %concatenate.7.refs_0_), channel_id=1, source_target_pairs={{0,64},{64,128},{128,192},{192,0},{1,65},{65,129},{129,193},{193,1... | collective-permute-start | bytes 356360 | tf_op jit(solution)/shard_map/ppermute | solution.py:25
  12.1 5.2 %collective-permute-start = (bf16[16,3584]{1,0:T(8,128)(2,1)S(1)}, bf16[16,3584]{1,0:T(8,128)(2,1)S(1)}, u32[]{:S(2)}, u32[]{:S(2)}) collective-permute-start(bf16[16,3584]{1,0:T(8,128)(2,1)S(1)} %get-tuple-element.35.refs_0_), channel_id=1, source_target_pairs={{0,8},{8,16},{16,24},{24,32},{32,40},{40,48},{48,56},{56,0},{1,9},... | collective-permute-start | bytes 344072 | tf_op jit(solution)/shard_map/ppermute | solution.py:25
  12.1 6.7 %collective-permute-start.16 = (bf16[16,3712]{1,0:T(8,128)(2,1)S(1)}, bf16[16,3712]{1,0:T(8,128)(2,1)S(1)}, u32[]{:S(2)}, u32[]{:S(2)}) collective-permute-start(bf16[16,3712]{1,0:T(8,128)(2,1)S(1)} %concatenate.7.refs_0_), channel_id=1, source_target_pairs={{0,192},{64,0},{128,64},{192,128},{1,193},{65,1},{129,65},{193,129... | collective-permute-start | bytes 356360 | tf_op jit(solution)/shard_map/ppermute | solution.py:25
  13.6 6.4 %collective-permute-start.17 = (bf16[16,3712]{1,0:T(8,128)(2,1)S(1)}, bf16[16,3712]{1,0:T(8,128)(2,1)S(1)}, u32[]{:S(2)}, u32[]{:S(2)}) collective-permute-start(bf16[16,3712]{1,0:T(8,128)(2,1)S(1)} %concatenate.7.refs_0_), channel_id=1, source_target_pairs={{0,128},{64,192},{128,0},{192,64},{1,129},{65,193},{129,1},{193,65... | collective-permute-start | bytes 356360 | tf_op jit(solution)/shard_map/ppermute | solution.py:25
  17.4 11.2 %copy-start.16 = (bf16[16,3584]{1,0:T(8,128)(2,1)}, bf16[16,3584]{1,0:T(8,128)(2,1)S(1)}, u32[]{:S(2)}) copy-start(bf16[16,3584]{1,0:T(8,128)(2,1)S(1)} %collective-permute-done.refs_1_) | copy-start | bytes 344068
  17.4 3.6 %collective-permute-start.3 = (bf16[16,3584]{1,0:T(8,128)(2,1)S(1)}, bf16[16,3584]{1,0:T(8,128)(2,1)S(1)}, u32[]{:S(2)}, u32[]{:S(2)}) collective-permute-start(bf16[16,3584]{1,0:T(8,128)(2,1)S(1)} %collective-permute-done.1.refs_2_), channel_id=1, source_target_pairs={{0,56},{8,0},{16,8},{24,16},{32,24},{40,32},{48,40},{56,48},{1,57}... | collective-permute-start | bytes 344072 | tf_op jit(solution)/shard_map/ppermute | solution.py:25
  17.8 5.8 %collective-permute-start.2 = (bf16[16,3584]{1,0:T(8,128)(2,1)S(1)}, bf16[16,3584]{1,0:T(8,128)(2,1)S(1)}, u32[]{:S(2)}, u32[]{:S(2)}) collective-permute-start(bf16[16,3584]{1,0:T(8,128)(2,1)S(1)} %collective-permute-done.refs_1_), channel_id=1, source_target_pairs={{0,8},{8,16},{16,24},{24,32},{32,40},{40,48},{48,56},{56,0},{1,9},... | collective-permute-start | bytes 344072 | tf_op jit(solution)/shard_map/ppermute | solution.py:25
  20.1 68.9 %copy-start.6 = (bf16[2,16,3712]{2,1,0:T(8,128)(2,1)}, bf16[2,16,3712]{2,1,0:T(8,128)(2,1)S(1)}, u32[]{:S(2)}) copy-start(bf16[2,16,3712]{2,1,0:T(8,128)(2,1)S(1)} %get-tuple-element.21.refs_1_) | copy-start | bytes 712708
  20.1 15.2 %collective-permute-start.18 = (bf16[2,16,3712]{2,1,0:T(8,128)(2,1)S(1)}, bf16[2,16,3712]{2,1,0:T(8,128)(2,1)S(1)}, u32[]{:S(2)}, u32[]{:S(2)}) collective-permute-start(bf16[2,16,3712]{2,1,0:T(8,128)(2,1)S(1)} %get-tuple-element.20.refs_0_), channel_id=1, source_target_pairs={{0,8},{8,16},{16,24},{24,32},{32,40},{40,48},{48,56},{56,0},{1,9},... | collective-permute-start | bytes 712712 | tf_op jit(solution)/shard_map/ppermute | solution.py:25
  21.0 11.0 %collective-permute-start.5 = (bf16[16,3584]{1,0:T(8,128)(2,1)S(1)}, bf16[16,3584]{1,0:T(8,128)(2,1)S(1)}, u32[]{:S(2)}, u32[]{:S(2)}) collective-permute-start(bf16[16,3584]{1,0:T(8,128)(2,1)S(1)} %collective-permute-done.3.refs_4_), channel_id=1, source_target_pairs={{0,56},{8,0},{16,8},{24,16},{32,24},{40,32},{48,40},{56,48},{1,57}... | collective-permute-start | bytes 344072 | tf_op jit(solution)/shard_map/ppermute | solution.py:25
  23.6 8.4 %collective-permute-start.4 = (bf16[16,3584]{1,0:T(8,128)(2,1)S(1)}, bf16[16,3584]{1,0:T(8,128)(2,1)S(1)}, u32[]{:S(2)}, u32[]{:S(2)}) collective-permute-start(bf16[16,3584]{1,0:T(8,128)(2,1)S(1)} %collective-permute-done.2.refs_3_), channel_id=1, source_target_pairs={{0,8},{8,16},{16,24},{24,32},{32,40},{40,48},{48,56},{56,0},{1,9},... | collective-permute-start | bytes 344072 | tf_op jit(solution)/shard_map/ppermute | solution.py:25
  24.3 4.2 %collective-permute-start.14 = (bf16[2,128,128]{2,1,0:T(8,128)(2,1)S(1)}, bf16[2,128,128]{2,1,0:T(8,128)(2,1)S(1)}, u32[]{:S(2)}, u32[]{:S(2)}) collective-permute-start(bf16[2,128,128]{2,1,0:T(8,128)(2,1)S(1)} %bitcast.30), channel_id=1, source_target_pairs={{0,4},{4,0},{1,5},{5,1},{2,6},{6,2},{3,7},{7,3},{8,12},{12,8},{9,1... | collective-permute-start | bytes 196616 | tf_op jit(solution)/shard_map/ppermute | solution.py:25
  29.1 7.6 %collective-permute-start.20 = (bf16[2,16,3712]{2,1,0:T(8,128)(2,1)S(1)}, bf16[2,16,3712]{2,1,0:T(8,128)(2,1)S(1)}, u32[]{:S(2)}, u32[]{:S(2)}) collective-permute-start(bf16[2,16,3712]{2,1,0:T(8,128)(2,1)S(1)} %get-tuple-element.21.refs_1_), channel_id=1, source_target_pairs={{0,56},{8,0},{16,8},{24,16},{32,24},{40,32},{48,40},{56,48},{1,57}... | collective-permute-start | bytes 712712 | tf_op jit(solution)/shard_map/ppermute | solution.py:25
  32.0 8.8 %collective-permute-start.19 = (bf16[2,16,3712]{2,1,0:T(8,128)(2,1)S(1)}, bf16[2,16,3712]{2,1,0:T(8,128)(2,1)S(1)}, u32[]{:S(2)}, u32[]{:S(2)}) collective-permute-start(bf16[2,16,3712]{2,1,0:T(8,128)(2,1)S(1)} %get-tuple-element.21.refs_1_), channel_id=1, source_target_pairs={{0,8},{8,16},{16,24},{24,32},{32,40},{40,48},{48,56},{56,0},{1,9},... | collective-permute-start | bytes 712712 | tf_op jit(solution)/shard_map/ppermute | solution.py:25
  32.6 9.2 %collective-permute-start.21 = (bf16[2,16,3712]{2,1,0:T(8,128)(2,1)S(1)}, bf16[2,16,3712]{2,1,0:T(8,128)(2,1)}, u32[]{:S(2)}, u32[]{:S(2)}) collective-permute-start(bf16[2,16,3712]{2,1,0:T(8,128)(2,1)S(1)} %get-tuple-element.20.refs_0_), channel_id=1, source_target_pairs={{0,56},{8,0},{16,8},{24,16},{32,24},{40,32},{48,40},{56,48},{1,57}... | collective-permute-start | bytes 712712 | tf_op jit(solution)/shard_map/ppermute | solution.py:25
  35.3 14.9 %copy-start.8 = (bf16[2,16,3712]{2,1,0:T(8,128)(2,1)}, bf16[2,16,3712]{2,1,0:T(8,128)(2,1)S(1)}, u32[]{:S(2)}) copy-start(bf16[2,16,3712]{2,1,0:T(8,128)(2,1)S(1)} %collective-permute-done.18.refs_2_) | copy-start | bytes 712708
  35.3 13.1 %collective-permute-start.22 = (bf16[2,16,3712]{2,1,0:T(8,128)(2,1)S(1)}, bf16[2,16,3712]{2,1,0:T(8,128)(2,1)}, u32[]{:S(2)}, u32[]{:S(2)}) collective-permute-start(bf16[2,16,3712]{2,1,0:T(8,128)(2,1)S(1)} %collective-permute-done.18.refs_2_), channel_id=1, source_target_pairs={{0,8},{8,16},{16,24},{24,32},{32,40},{40,48},{48,56},{56,0},{1,9},... | collective-permute-start | bytes 712712 | tf_op jit(solution)/shard_map/ppermute | solution.py:25
  36.7 52.2 %copy-start.10 = (bf16[2,16,3712]{2,1,0:T(8,128)(2,1)}, bf16[2,16,3712]{2,1,0:T(8,128)(2,1)S(1)}, u32[]{:S(2)}) copy-start(bf16[2,16,3712]{2,1,0:T(8,128)(2,1)S(1)} %collective-permute-done.20.refs_4_) | copy-start | bytes 712708
  36.7 7.5 %collective-permute-start.6 = (bf16[16,3584]{1,0:T(8,128)(2,1)S(1)}, bf16[16,3584]{1,0:T(8,128)(2,1)S(1)}, u32[]{:S(2)}, u32[]{:S(2)}) collective-permute-start(bf16[16,3584]{1,0:T(8,128)(2,1)S(1)} %collective-permute-done.5.refs_6_), channel_id=1, source_target_pairs={{0,56},{8,0},{16,8},{24,16},{32,24},{40,32},{48,40},{56,48},{1,57}... | collective-permute-start | bytes 344072 | tf_op jit(solution)/shard_map/ppermute | solution.py:25
  40.8 48.2 %copy-start.12 = (bf16[2,16,3712]{2,1,0:T(8,128)(2,1)}, bf16[2,16,3712]{2,1,0:T(8,128)(2,1)S(1)}, u32[]{:S(2)}) copy-start(bf16[2,16,3712]{2,1,0:T(8,128)(2,1)S(1)} %collective-permute-done.19.refs_3_) | copy-start | bytes 712708
  40.8 15.4 %collective-permute-start.24 = (bf16[2,16,3712]{2,1,0:T(8,128)(2,1)S(1)}, bf16[2,16,3712]{2,1,0:T(8,128)(2,1)}, u32[]{:S(2)}, u32[]{:S(2)}) collective-permute-start(bf16[2,16,3712]{2,1,0:T(8,128)(2,1)S(1)} %collective-permute-done.20.refs_4_), channel_id=1, source_target_pairs={{0,56},{8,0},{16,8},{24,16},{32,24},{40,32},{48,40},{56,48},{1,57}... | collective-permute-start | bytes 712712 | tf_op jit(solution)/shard_map/ppermute | solution.py:25
  41.8 16.9 %collective-permute-start.23 = (bf16[2,16,3712]{2,1,0:T(8,128)(2,1)S(1)}, bf16[2,16,3712]{2,1,0:T(8,128)(2,1)}, u32[]{:S(2)}, u32[]{:S(2)}) collective-permute-start(bf16[2,16,3712]{2,1,0:T(8,128)(2,1)S(1)} %collective-permute-done.19.refs_3_), channel_id=1, source_target_pairs={{0,8},{8,16},{16,24},{24,32},{32,40},{40,48},{48,56},{56,0},{1,9},... | collective-permute-start | bytes 712712 | tf_op jit(solution)/shard_map/ppermute | solution.py:25
  44.9 20.2 %collective-permute-start.25 = (bf16[2,16,3712]{2,1,0:T(8,128)(2,1)}, bf16[2,16,3712]{2,1,0:T(8,128)(2,1)}, u32[]{:S(2)}, u32[]{:S(2)}) collective-permute-start(bf16[2,16,3712]{2,1,0:T(8,128)(2,1)} %collective-permute-done.21.refs_5_), channel_id=1, source_target_pairs={{0,56},{8,0},{16,8},{24,16},{32,24},{40,32},{48,40},{56,48},{1,57}... | collective-permute-start | bytes 712712 | tf_op jit(solution)/shard_map/ppermute | solution.py:25
  48.4 18.0 %collective-permute-start.26 = (bf16[2,16,3712]{2,1,0:T(8,128)(2,1)}, bf16[2,16,3712]{2,1,0:T(8,128)(2,1)}, u32[]{:S(2)}, u32[]{:S(2)}) collective-permute-start(bf16[2,16,3712]{2,1,0:T(8,128)(2,1)} %collective-permute-done.22.refs_6_), channel_id=1, source_target_pairs={{0,8},{8,16},{16,24},{24,32},{32,40},{40,48},{48,56},{56,0},{1,9},... | collective-permute-start | bytes 712712 | tf_op jit(solution)/shard_map/ppermute | solution.py:25
  50.2 40.6 %all-to-all-start = ((bf16[1,16,32,256]{3,1,0,2:T(8,128)(2,1)}), bf16[1,16,32,256]{3,1,0,2:T(8,128)(2,1)S(1)}, u32[]{:S(2)}, u32[]{:S(2)}) async-start(bf16[1,16,32,256]{3,1,0,2:T(8,128)(2,1)} %copy.18), calls=%async_computation | async-start | bytes 524288 | tf_op jit(solution)/shard_map/all_to_all | solution.py:198
  56.2 11.7 %collective-permute-start.28 = (bf16[2,16,3712]{2,1,0:T(8,128)(2,1)}, bf16[2,16,3712]{2,1,0:T(8,128)(2,1)}, u32[]{:S(2)}, u32[]{:S(2)}) collective-permute-start(bf16[2,16,3712]{2,1,0:T(8,128)(2,1)} %collective-permute-done.24.refs_8_), channel_id=1, source_target_pairs={{0,56},{8,0},{16,8},{24,16},{32,24},{40,32},{48,40},{56,48},{1,57}... | collective-permute-start | bytes 712712 | tf_op jit(solution)/shard_map/ppermute | solution.py:25
  58.7 11.9 %collective-permute-start.27 = (bf16[2,16,3712]{2,1,0:T(8,128)(2,1)}, bf16[2,16,3712]{2,1,0:T(8,128)(2,1)S(1)}, u32[]{:S(2)}, u32[]{:S(2)}) collective-permute-start(bf16[2,16,3712]{2,1,0:T(8,128)(2,1)} %collective-permute-done.23.refs_7_), channel_id=1, source_target_pairs={{0,8},{8,16},{16,24},{24,32},{32,40},{40,48},{48,56},{56,0},{1,9},... | collective-permute-start | bytes 712712 | tf_op jit(solution)/shard_map/ppermute | solution.py:25
  58.8 0.9 copy-start.17
  59.7 0.9 copy-start.19
  60.6 0.9 copy-start.21
  61.5 0.9 copy-start.23
  62.4 0.9 copy-start.25
  63.3 0.9 copy-start.27
  65.2 11.2 %collective-permute-start.7 = (bf16[4,16,3584]{2,1,0:T(8,128)(2,1)}, bf16[4,16,3584]{2,1,0:T(8,128)(2,1)}, u32[]{:S(2)}, u32[]{:S(2)}) collective-permute-start(bf16[4,16,3584]{2,1,0:T(8,128)(2,1)} %get-tuple-element.18.refs_0_), channel_id=1, source_target_pairs={{0,64},{64,128},{128,192},{192,0},{1,65},{65,129},{129,193},{193,1... | collective-permute-start | bytes 1376264 | tf_op jit(solution)/shard_map/ppermute | solution.py:25
  66.4 10.6 %collective-permute-start.10 = (bf16[4,16,3584]{2,1,0:T(8,128)(2,1)}, bf16[4,16,3584]{2,1,0:T(8,128)(2,1)}, u32[]{:S(2)}, u32[]{:S(2)}) collective-permute-start(bf16[4,16,3584]{2,1,0:T(8,128)(2,1)} %get-tuple-element.19.refs_1_), channel_id=1, source_target_pairs={{0,192},{64,0},{128,64},{192,128},{1,193},{65,1},{129,65},{193,129... | collective-permute-start | bytes 1376264 | tf_op jit(solution)/shard_map/ppermute | solution.py:25
  67.9 6.0 %collective-permute-start.29 = (bf16[2,16,3712]{2,1,0:T(8,128)(2,1)}, bf16[2,16,3712]{2,1,0:T(8,128)(2,1)}, u32[]{:S(2)}, u32[]{:S(2)}) collective-permute-start(bf16[2,16,3712]{2,1,0:T(8,128)(2,1)} %collective-permute-done.25.refs_9_), channel_id=1, source_target_pairs={{0,56},{8,0},{16,8},{24,16},{32,24},{40,32},{48,40},{56,48},{1,57}... | collective-permute-start | bytes 712712 | tf_op jit(solution)/shard_map/ppermute | solution.py:25
  71.3 8.8 %collective-permute-start.30 = (bf16[2,16,3712]{2,1,0:T(8,128)(2,1)}, bf16[2,16,3712]{2,1,0:T(8,128)(2,1)}, u32[]{:S(2)}, u32[]{:S(2)}) collective-permute-start(bf16[2,16,3712]{2,1,0:T(8,128)(2,1)} %collective-permute-done.26.refs_10_), channel_id=1, source_target_pairs={{0,8},{8,16},{16,24},{24,32},{32,40},{40,48},{48,56},{56,0},{1,9},... | collective-permute-start | bytes 712712 | tf_op jit(solution)/shard_map/ppermute | solution.py:25
  74.0 34.5 %collective-permute-start.8 = (bf16[4,16,3584]{2,1,0:T(8,128)(2,1)}, bf16[4,16,3584]{2,1,0:T(8,128)(2,1)}, u32[]{:S(2)}, u32[]{:S(2)}) collective-permute-start(bf16[4,16,3584]{2,1,0:T(8,128)(2,1)} %get-tuple-element.19.refs_1_), channel_id=1, source_target_pairs={{0,64},{64,128},{128,192},{192,0},{1,65},{65,129},{129,193},{193,1... | collective-permute-start | bytes 1376264 | tf_op jit(solution)/shard_map/ppermute | solution.py:25
  76.4 32.1 %collective-permute-start.9 = (bf16[4,16,3584]{2,1,0:T(8,128)(2,1)}, bf16[4,16,3584]{2,1,0:T(8,128)(2,1)}, u32[]{:S(2)}, u32[]{:S(2)}) collective-permute-start(bf16[4,16,3584]{2,1,0:T(8,128)(2,1)} %get-tuple-element.18.refs_0_), channel_id=1, source_target_pairs={{0,192},{64,0},{128,64},{192,128},{1,193},{65,1},{129,65},{193,129... | collective-permute-start | bytes 1376264 | tf_op jit(solution)/shard_map/ppermute | solution.py:25
  77.0 13.9 %collective-permute-start.31 = (bf16[2,16,3712]{2,1,0:T(8,128)(2,1)}, bf16[2,16,3712]{2,1,0:T(8,128)(2,1)}, u32[]{:S(2)}, u32[]{:S(2)}) collective-permute-start(bf16[2,16,3712]{2,1,0:T(8,128)(2,1)} %collective-permute-done.28.refs_12_), channel_id=1, source_target_pairs={{0,56},{8,0},{16,8},{24,16},{32,24},{40,32},{48,40},{56,48},{1,57}... | collective-permute-start | bytes 712712 | tf_op jit(solution)/shard_map/ppermute | solution.py:25
  80.1 28.4 %collective-permute-start.11 = (bf16[4,16,3584]{2,1,0:T(8,128)(2,1)}, bf16[4,16,3584]{2,1,0:T(8,128)(2,1)}, u32[]{:S(2)}, u32[]{:S(2)}) collective-permute-start(bf16[4,16,3584]{2,1,0:T(8,128)(2,1)} %collective-permute-done.7.refs_2_), channel_id=1, source_target_pairs={{0,64},{64,128},{128,192},{192,0},{1,65},{65,129},{129,193},{193,1... | collective-permute-start | bytes 1376264 | tf_op jit(solution)/shard_map/ppermute | solution.py:25
  80.1 28.4 %collective-permute-start.12 = (bf16[4,16,3584]{2,1,0:T(8,128)(2,1)}, bf16[4,16,3584]{2,1,0:T(8,128)(2,1)}, u32[]{:S(2)}, u32[]{:S(2)}) collective-permute-start(bf16[4,16,3584]{2,1,0:T(8,128)(2,1)} %collective-permute-done.10.refs_5_), channel_id=1, source_target_pairs={{0,192},{64,0},{128,64},{192,128},{1,193},{65,1},{129,65},{193,129... | collective-permute-start | bytes 1376264 | tf_op jit(solution)/shard_map/ppermute | solution.py:25
  83.1 1.5 %copy-start.5 = (bf16[7168,128]{1,0:T(8,128)(2,1)S(1)}, bf16[7168,128]{1,0:T(8,128)(2,1)}, u32[]{:S(2)}) copy-start(bf16[7168,128]{1,0:T(8,128)(2,1)} %w_ref.1) | copy-start | bytes 5505028
  84.6 0.8 copy-start.29
  85.4 0.8 copy-start.31
  89.0 1.8 %copy-start.1 = (bf16[7168,256]{1,0:T(8,128)(2,1)}, bf16[7168,256]{1,0:T(8,128)(2,1)S(1)}, u32[]{:S(2)}) copy-start(bf16[7168,256]{1,0:T(8,128)(2,1)S(1)} %prep.1.refs_16_.refs_8_) | copy-start | bytes 11010052
  90.8 2.0 %copy-start.2 = (bf16[7168,256]{1,0:T(8,128)(2,1)S(1)}, bf16[7168,256]{1,0:T(8,128)(2,1)}, u32[]{:S(2)}) copy-start(bf16[7168,256]{1,0:T(8,128)(2,1)} %copy-done.1) | copy-start | bytes 11010052
  92.9 0.9 copy-start.7
  93.8 0.9 copy-start.9
  94.8 0.9 copy-start.11
  95.7 0.9 copy-start.13
  96.6 0.9 copy-start.15
  97.6 10.9 %copy-start.3 = (bf16[7168,256]{1,0:T(8,128)(2,1)S(1)}, bf16[7168,256]{1,0:T(8,128)(2,1)}, u32[]{:S(2)}) copy-start(bf16[7168,256]{1,0:T(8,128)(2,1)} %copy-done.1) | copy-start | bytes 11010052
  101.9 26.4 %collective-permute-start.32 = (f32[64,3584]{1,0:T(8,128)S(1)}, f32[64,3584]{1,0:T(8,128)}, u32[]{:S(2)}, u32[]{:S(2)}) collective-permute-start(f32[64,3584]{1,0:T(8,128)S(1)} %get-tuple-element.28.x_ref), channel_id=1, source_target_pairs={{0,4},{4,0},{1,5},{5,1},{2,6},{6,2},{3,7},{7,3},{8,12},{12,8},{9,1... | collective-permute-start | bytes 2752520 | tf_op jit(solution)/shard_map/ppermute | solution.py:25
  114.5 15.8 %collective-permute-start.33 = (f32[64,3584]{1,0:T(8,128)}, f32[64,3584]{1,0:T(8,128)}, u32[]{:S(2)}, u32[]{:S(2)}) collective-permute-start(f32[64,3584]{1,0:T(8,128)} %get-tuple-element.29.x_ref), channel_id=1, source_target_pairs={{0,4},{4,0},{1,5},{5,1},{2,6},{6,2},{3,7},{7,3},{8,12},{12,8},{9,1... | collective-permute-start | bytes 2752520 | tf_op jit(solution)/shard_map/ppermute | solution.py:25
  114.5 5.2 %collective-permute-start.34 = (f32[2,128,128]{2,1,0:T(8,128)S(1)}, f32[2,128,128]{2,1,0:T(8,128)S(1)}, u32[]{:S(2)}, u32[]{:S(2)}) collective-permute-start(f32[2,128,128]{2,1,0:T(8,128)S(1)} %slice.19), channel_id=1, source_target_pairs={{0,4},{4,0},{1,5},{5,1},{2,6},{6,2},{3,7},{7,3},{8,12},{12,8},{9,1... | collective-permute-start | bytes 393224 | tf_op jit(solution)/shard_map/ppermute | solution.py:25
  115.1 12.5 %all-to-all-start.1 = ((bf16[8,192,128]{2,1,0:T(8,128)(2,1)}), bf16[8,192,128]{2,1,0:T(8,128)(2,1)S(1)}, u32[]{:S(2)}, u32[]{:S(2)}) async-start(bf16[8,192,128]{2,1,0:T(8,128)(2,1)} %get-tuple-element.26), calls=%async_computation.1 | async-start | bytes 786432 | tf_op jit(solution)/shard_map/all_to_all | solution.py:244
  (7 other events, 4.5 us)
